TPU v7x, 256 devices: a whole 4x4x8 slice. The times are simulated.
256 devices in a mesh: dp: 8 (over x, core), ctx: 32 (over y, z).
Axes of the slice: x: 4, y: 4, z: 8, core: 2. Of those that a mesh axis runs over, the one named last changes fastest.
Arguments:
- tokens: bfloat16 [32768, 4096], P(('dp', 'ctx')), parts along dimension 0, may hold values from -6 to 6
- pick_flags: int32 [32768], P(('dp', 'ctx')), parts along dimension 0, may hold values from 0 to 1, as said below
- gate_scales: bfloat16 [32768], P(('dp', 'ctx')), parts along dimension 0, may hold values from 0.099609375 to 1
- attn_gain: float32 [4096], replicated, may hold values from 0.4 to 1.6
- query_weight: bfloat16 [4096, 4096], P(None, 'ctx')
- key_weight: bfloat16 [4096, 1024], P(None, 'ctx')
- value_matrix: bfloat16 [4096, 1024], P(None, 'ctx'), may hold values from -0.09375 to 0.09375
- output_weight: bfloat16 [4096, 4096], P('ctx'), may hold values from -0.09375 to 0.09375
- ffn_gain: float32 [4096], replicated, may hold values from 0.25 to 1.75
- gate_weight: bfloat16 [4096, 11264], P(None, 'ctx'), may hold values from -0.09375 to 0.09375
- up_weight: bfloat16 [4096, 11264], P(None, 'ctx'), may hold values from -0.09375 to 0.09375
- down_weight: bfloat16 [11264, 4096], P('ctx'), may hold values from -0.0546875 to 0.0546875
Outputs:
- block_out: bfloat16 [32768, 4096], P(('dp', 'ctx')), parts along dimension 0
There are 8 independent parts, one for each index of `dp`. A program takes and returns all parts, laid end to end along the dimension named above; an argument that names none is the same for every part. Nothing has to cross between parts.
Inputs may be any that keep to these rules, and one draw needn't show every extreme that they name: `pick_flags`: each device's 128 tokens hold at most 32 picks, the first device exactly 32; each document holds exactly 512 picks; a device may hold none.
All inputs are finite; a program needn't handle non-finite values.
Results may differ from a plain program's by a relative error of at most 0.01.
Values may be sent and summed in bfloat16 or wider, within the bound.
A program may use at most 128 MiB of HBM per device.

v0:
```python
import jax
import jax.numpy as jnp
from jax import lax
from jax.sharding import PartitionSpec as P

QUERY_HEADS = 32
KEY_VALUE_HEADS = 8
HEAD_SIZE = 128
PICK_DEV = 16
MOST = 32


norm_eps = 1e-05
rope_base = 500000.0


def rms_scale(matrix, gain_vec):
    mean_square = jnp.mean(matrix * matrix, axis=-1, keepdims=True)
    return matrix * lax.rsqrt(mean_square + norm_eps) * gain_vec


def apply_rotary(values, token_positions):
    half_dim = values.shape[-1] // 2
    frequency = rope_base ** (-(jnp.arange(half_dim, dtype=jnp.float32) * 2.0) / values.shape[-1])
    angles = token_positions.astype(jnp.float32)[:, None] * frequency[None, :]
    cosine = jnp.cos(angles)[:, None, :]
    sine_part = jnp.sin(angles)[:, None, :]
    lower_half = values[..., :half_dim]
    upper_half = values[..., half_dim:]
    return jnp.concatenate(
        (
            lower_half * cosine - upper_half * sine_part,
            upper_half * cosine + lower_half * sine_part,
        ),
        axis=-1,
    )


def body(
    tokens,
    pick_flags,
    gate_scales,
    attn_gain,
    query_weight,
    key_weight,
    value_matrix,
    output_weight,
    ffn_gain,
    gate_weight,
    up_weight,
    down_weight,
):
    tok_local = tokens.shape[0]
    ctx_size = lax.axis_size("ctx")
    my_index = lax.axis_index("ctx")
    picked_count = PICK_DEV * ctx_size
    half_pick = PICK_DEV // 2
    half_cycle = ctx_size // 2
    slot_of = jnp.cumsum(pick_flags) - 1
    token_ids = jnp.arange(tok_local, dtype=jnp.int32)
    slot_match = (jnp.arange(MOST, dtype=jnp.int32)[:, None] == slot_of[None, :]) & (
        pick_flags[None, :] == 1
    )
    chosen = jnp.sum(jnp.where(slot_match, token_ids[None, :], 0), axis=1)
    filled = jnp.any(slot_match, axis=1)
    local_index = jnp.where(filled, chosen, -1)
    padded_rows = jnp.where(filled[:, None], tokens[chosen], jnp.zeros((), jnp.bfloat16))
    padded_gate = jnp.where(filled, gate_scales[chosen], jnp.zeros((), jnp.bfloat16))
    all_rows, all_gate, all_index = (
        lax.all_gather(padded_rows, "ctx", axis=0, tiled=True),
        lax.all_gather(padded_gate, "ctx", axis=0, tiled=True),
        lax.all_gather(local_index, "ctx", axis=0, tiled=True),
    )
    counts = jnp.sum((all_index >= 0).reshape(ctx_size, MOST).astype(jnp.int32), axis=1)
    run_ends = jnp.cumsum(counts)
    run_starts = run_ends - counts
    order_ids = jnp.arange(picked_count, dtype=jnp.int32)
    owner_of = order_ids // PICK_DEV
    within = order_ids % PICK_DEV
    low_part = within < half_pick
    rank_block = jnp.where(low_part, owner_of, (owner_of + half_cycle) % ctx_size)
    rank_inner = jnp.where(low_part, 2 * within, 2 * (within - half_pick) + 1)
    rank_ids = rank_block * PICK_DEV + rank_inner
    source = jnp.sum((run_ends[None, :] <= rank_ids[:, None]).astype(jnp.int32), axis=1)
    flat_row = source * MOST + rank_ids - run_starts[source]
    picked_rows = all_rows[flat_row]
    scales = all_gate[flat_row].astype(jnp.float32)
    token_positions = source * tok_local + all_index[flat_row]
    normalized_rows = rms_scale(picked_rows.astype(jnp.float32), attn_gain).astype(jnp.bfloat16)
    heads_here = query_weight.shape[1] // HEAD_SIZE
    queries = jnp.dot(normalized_rows, query_weight, preferred_element_type=jnp.float32).reshape(
        picked_count, heads_here, HEAD_SIZE
    )
    queries = apply_rotary(queries, token_positions).astype(jnp.bfloat16)
    kv_weight = jnp.concatenate((key_weight, value_matrix), axis=1)
    kv_local = jnp.einsum(
        "pd,dc->cp", normalized_rows, kv_weight, preferred_element_type=jnp.float32
    ).astype(jnp.bfloat16)
    kv_all = lax.all_gather(kv_local, "ctx", axis=0, tiled=True)
    col_count = key_weight.shape[1]
    key_value_parts = kv_all.reshape(ctx_size, 2, col_count, picked_count)
    key_columns = key_value_parts[:, 0].reshape(HEAD_SIZE * KEY_VALUE_HEADS, picked_count)
    value_columns = key_value_parts[:, 1].reshape(HEAD_SIZE * KEY_VALUE_HEADS, picked_count)
    key_heads = jnp.transpose(
        key_columns.T.astype(jnp.float32).reshape(picked_count, HEAD_SIZE, KEY_VALUE_HEADS),
        (0, 2, 1),
    )
    rotated_keys = apply_rotary(key_heads, token_positions).astype(jnp.bfloat16)
    repeated_values = jnp.transpose(
        value_columns.T.reshape(picked_count, HEAD_SIZE, KEY_VALUE_HEADS), (0, 2, 1)
    )
    query_group_width = QUERY_HEADS // KEY_VALUE_HEADS
    kv_pick = (my_index * heads_here + jnp.arange(heads_here, dtype=jnp.int32)) // query_group_width
    keys_here = jnp.take(rotated_keys, kv_pick, axis=1)
    values_here = jnp.take(repeated_values, kv_pick, axis=1)
    scores = jnp.einsum(
        "qhd,khd->hqk", queries, keys_here, preferred_element_type=jnp.float32
    ) / jnp.sqrt(jnp.float32(HEAD_SIZE))
    allowed = token_positions[None, :] <= token_positions[:, None]
    scores = jnp.where(allowed[None, :, :], scores, -jnp.inf)
    row_max = jnp.max(scores, axis=2, keepdims=True)
    exp_terms = jnp.exp(scores - row_max)
    prob_bf = (exp_terms / jnp.sum(exp_terms, axis=2, keepdims=True)).astype(jnp.bfloat16)
    head_out = jnp.einsum(
        "hqk,khd->qhd", prob_bf, values_here, preferred_element_type=jnp.float32
    ).astype(jnp.bfloat16)
    head_out = head_out.reshape(picked_count, heads_here * HEAD_SIZE)
    own_start = my_index * PICK_DEV
    own_rows = lax.dynamic_slice_in_dim(picked_rows, own_start, PICK_DEV, 0).astype(jnp.float32)
    row_block = head_out
    attn_own = lax.psum_scatter(
        jnp.dot(row_block, output_weight, preferred_element_type=jnp.float32).astype(jnp.bfloat16),
        "ctx",
        scatter_dimension=0,
        tiled=True,
    ).astype(jnp.float32)
    mixed_own = own_rows + attn_own
    normed_own = rms_scale(mixed_own, ffn_gain).astype(jnp.bfloat16)
    normed_ffn = lax.all_gather(normed_own, "ctx", axis=0, tiled=True)
    row_block = normed_ffn
    gate_proj = jnp.dot(row_block, gate_weight, preferred_element_type=jnp.float32)
    up_proj = jnp.dot(row_block, up_weight, preferred_element_type=jnp.float32)
    hidden = (jax.nn.silu(gate_proj) * up_proj).astype(jnp.bfloat16)
    ffn_own = lax.psum_scatter(
        jnp.dot(hidden, down_weight, preferred_element_type=jnp.float32).astype(jnp.bfloat16),
        "ctx",
        scatter_dimension=0,
        tiled=True,
    ).astype(jnp.float32)
    scale_own = lax.dynamic_slice_in_dim(scales, own_start, PICK_DEV, 0)
    final_own = (own_rows + scale_own[:, None] * (attn_own + ffn_own)).astype(jnp.bfloat16)
    final_all = lax.all_gather(final_own, "ctx", axis=0, tiled=True)
    my_start = run_starts[my_index]
    rank_here = jnp.clip(my_start + slot_of, 0, picked_count - 1)
    inner_here = rank_here % PICK_DEV
    odd_here = inner_here % 2
    owner_here = (rank_here // PICK_DEV + odd_here * half_cycle) % ctx_size
    take_rows = owner_here * PICK_DEV + inner_here // 2 + odd_here * half_pick
    return jnp.where(pick_flags[:, None] == 1, final_all[take_rows], tokens)


def solution(mesh):
    in_specs = (
        P(("dp", "ctx"), None),
        P(("dp", "ctx")),
        P(("dp", "ctx")),
        P(),
        P(None, "ctx"),
        P(None, "ctx"),
        P(None, "ctx"),
        P("ctx", None),
        P(),
        P(None, "ctx"),
        P(None, "ctx"),
        P("ctx", None),
    )
    out_specs = P(("dp", "ctx"), None)
    return jax.shard_map(body, mesh=mesh, in_specs=in_specs, out_specs=out_specs, check_vma=False)
```

profile of v0, /device:TPU:32, one launch (start us, length us, event | category | flops | bytes accessed | tf_op | source)
XLA Modules:
  0.0 852.4 jit_solution(5557066613425838501)
XLA Ops:
  8.7 2.3 gather_fusion
  13.8 22.9 %all-reduce = s32[1024]{0:T(1024)S(1)} all-reduce(s32[1024]{0:T(1024)S(1)} %select_dynamic-update-slice_fusion), channel_id=1, replica_groups=mesh['dp'=8,'ctx'=32] {'ctx'}, use_global_device_ids=true, to_apply=%add | all-reduce | flops 1024 | bytes 8192
  38.8 4.4 compare_select_fusion.5
  43.4 15.3 %select_select_fusion = s32[512]{0:T(512)S(1)} fusion(pred[512]{0:T(512)(128)(4,1)S(1)} %get-tuple-element.41, pred[512]{0:T(512)(128)(4,1)S(1)} %get-tuple-element.40, pred[512]{0:T(512)(128)(4,1)S(1)} %get-tuple-element.39, pred[512]{0:T(512)(128)(4,1)S(1)} %get-tuple-element.38, pred[512]{0:T(512)(128)(4,1)S(1)} %get-tuple-element.37, ...), kind=kLoop, calls=%fused_computation.169 | loop fusion | flops 12800 | bytes 16996 | tf_op jit(solution)/shard_map/gather | solution.py:85
  58.8 52.6 %all-gather.5.cloned.1.call-done = bf16[1024,4096]{1,0:T(8,128)(2,1)} async-done(((bf16[32,4096]{1,0:T(8,128)(2,1)}), bf16[1024,4096]{1,0:T(8,128)(2,1)}) %all-gather.5.cloned.1.call-update) | async-done | bytes 8388624 | tf_op jit(solution)/shard_map/all_gather | solution.py:70
  111.4 13.1 %gather_fusion.1 = bf16[512,4096]{1,0:T(8,128)(2,1)} fusion(bf16[1024,4096]{1,0:T(8,128)(2,1)} %all-gather.5.cloned.1.call-done, s32[1024]{0:T(1024)S(1)} %pad_clamp_fusion.1), kind=kCustom, calls=%fused_computation.1 | custom fusion | bytes 8390656 | tf_op jit(solution)/shard_map/gather | solution.py:86
  124.4 3.2 fusion
  127.9 3.0 fusion.13
  131.2 2.3 gather_fusion.4
  134.1 4.1 fusion.9
  139.4 67.6 %all-gather.7.cloned.1.call-done = bf16[2048,512]{1,0:T(8,128)(2,1)} async-done(((bf16[64,512]{1,0:T(8,128)(2,1)}), bf16[2048,512]{1,0:T(8,128)(2,1)}) %all-gather.7.cloned.1.call-update) | async-done | bytes 2097168 | tf_op jit(solution)/shard_map/all_gather | solution.py:99
  206.9 1.8 fusion.76
  213.6 5.1 convolution_convert_fusion
  218.8 218.4 %reduce-scatter.3.cloned.1.call-done = bf16[16,4096]{1,0:T(8,128)(2,1)} async-done(((bf16[512,4096]{1,0:T(8,128)(2,1)}), bf16[16,4096]{1,0:T(8,128)(2,1)}) %reduce-scatter.3.cloned.1.call-update) | async-done | bytes 131088 | tf_op jit(solution)/shard_map/reduce_scatter | solution.py:131
  440.1 81.2 %all-gather.9.cloned.1.call-done = bf16[512,4096]{1,0:T(8,128)(2,1)} async-done(((bf16[16,4096]{1,0:T(8,128)(2,1)}), bf16[512,4096]{1,0:T(8,128)(2,1)}) %all-gather.9.cloned.1.call-update) | async-done | bytes 4194320 | tf_op jit(solution)/shard_map/all_gather | solution.py:139
  521.3 5.6 fusion.80
  526.9 9.1 %convolution_convert_fusion.1 = bf16[512,4096]{1,0:T(8,128)(2,1)} fusion(bf16[352,4096]{1,0:T(8,128)(2,1)S(1)} %copy-done, bf16[512,4096]{1,0:T(8,128)(2,1)} %all-gather.9.cloned.1.call-done, bf16[4096,352]{0,1:T(8,128)(2,1)} %param.24, f32[512,352]{0,1:T(8,128)} %fusion.80), kind=kOutput, calls=%fused_computation.12 | convolution fusion | flops 2955968512 | bytes 14876672 | tf_op jit(solution)/shard_map/dot_general | solution.py:145
  537.7 70.0 %all-reduce.1 = bf16[1024]{0:T(1024)(128)(2,1)S(1)} all-reduce(bf16[1024]{0:T(1024)(128)(2,1)S(1)} %dynamic-update-slice.2), channel_id=1, replica_groups=mesh['dp'=8,'ctx'=32] {'ctx'}, use_global_device_ids=true, to_apply=%add.1 | all-reduce | flops 1024 | bytes 4096
  607.7 3.5 gather_fusion.3
  611.3 142.1 %reduce-scatter.5.cloned.1.call-done = bf16[16,4096]{1,0:T(8,128)(2,1)} async-done(((bf16[512,4096]{1,0:T(8,128)(2,1)}), bf16[16,4096]{1,0:T(8,128)(2,1)}) %reduce-scatter.5.cloned.1.call-update) | async-done | bytes 131088 | tf_op jit(solution)/shard_map/reduce_scatter | solution.py:144
  753.4 1.7 fusion.25
  756.1 80.9 %all-gather.11.cloned.1.call-done = bf16[512,4096]{1,0:T(8,128)(2,1)} async-done(((bf16[16,4096]{1,0:T(8,128)(2,1)}), bf16[512,4096]{1,0:T(8,128)(2,1)}) %all-gather.11.cloned.1.call-update) | async-done | bytes 4194320 | tf_op jit(solution)/shard_map/all_gather | solution.py:152
  837.0 5.9 gather_fusion.5
  842.9 2.7 broadcast_select_fusion
  (80 shorter events, 19.1 us)
Async XLA Ops:
  6.5 520.4 %copy-start = (bf16[352,4096]{1,0:T(8,128)(2,1)S(1)}, bf16[352,4096]{1,0:T(8,128)(2,1)}, u32[]{:S(2)}) copy-start(bf16[352,4096]{1,0:T(8,128)(2,1)} %param.25) | copy-start | bytes 8650756
  6.5 104.8 %all-gather.5.cloned.1.call-start = ((), (), s32[]{:S(2)}) async-start(), calls=%async_computation.2 | async-start | bytes 8650752 | tf_op jit(solution)/shard_map/all_gather | solution.py:70
  7.3 35.8 %copy-start.6 = (pred[128]{0:T(512)(128)(4,1)}, pred[128]{0:T(512)(128)(4,1)S(1)}, u32[]{:S(2)}) copy-start(pred[128]{0:T(512)(128)(4,1)S(1)} %broadcast_compare_fusion) | copy-start | bytes 388
  11.9 195.1 %all-gather.7.cloned.1.call-start = ((), (), s32[]{:S(2)}) async-start(), calls=%async_computation.3 | async-start | bytes 2162688 | tf_op jit(solution)/shard_map/all_gather | solution.py:99
  111.4 16.3 %copy-start.8 = (bf16[4096,32]{0,1:T(8,128)(2,1)S(1)}, bf16[4096,32]{0,1:T(8,128)(2,1)}, u32[]{:S(2)}) copy-start(bf16[4096,32]{0,1:T(8,128)(2,1)} %param.20) | copy-start | bytes 786436
  111.4 16.3 %copy-start.9 = (f32[4096]{0:T(1024)S(1)}, f32[4096]{0:T(1024)}, u32[]{:S(2)}) copy-start(f32[4096]{0:T(1024)} %param.17) | copy-start | bytes 49156
  124.4 3.4 copy-start.2
  130.9 306.2 %reduce-scatter.3.cloned.1.call-start = ((), (), s32[]{:S(2)}) async-start(), calls=%async_computation.4 | async-start | bytes 4325376 | tf_op jit(solution)/shard_map/reduce_scatter | solution.py:131
  212.4 1.0 copy-start.3
  213.6 224.7 %copy-start.5 = (f32[4096]{0:T(1024)S(1)}, f32[4096]{0:T(1024)}, u32[]{:S(2)}) copy-start(f32[4096]{0:T(1024)} %param.22) | copy-start | bytes 49156
  218.7 302.6 %all-gather.9.cloned.1.call-start = ((), (), s32[]{:S(2)}) async-start(), calls=%async_computation.5 | async-start | bytes 4325376 | tf_op jit(solution)/shard_map/all_gather | solution.py:139
  440.0 313.4 %reduce-scatter.5.cloned.1.call-start = ((), (), s32[]{:S(2)}) async-start(), calls=%async_computation.6 | async-start | bytes 4325376 | tf_op jit(solution)/shard_map/reduce_scatter | solution.py:144
  536.1 0.7 copy-start.1
  536.1 217.3 %copy-start.4 = (bf16[16,4096]{1,0:T(8,128)(2,1)S(1)}, bf16[16,4096]{1,0:T(8,128)(2,1)}, u32[]{:S(2)}) copy-start(bf16[16,4096]{1,0:T(8,128)(2,1)} %reduce-scatter.3.cloned.1.call-done) | copy-start | bytes 393220
  536.1 300.9 %all-gather.11.cloned.1.call-start = ((), (), s32[]{:S(2)}) async-start(), calls=%async_computation.7 | async-start | bytes 4325376 | tf_op jit(solution)/shard_map/all_gather | solution.py:152
  756.1 86.8 %copy-start.7 = (pred[128]{0:T(512)(128)(4,1)S(1)}, pred[128]{0:T(512)(128)(4,1)}, u32[]{:S(2)}) copy-start(pred[128]{0:T(512)(128)(4,1)} %copy-done.6) | copy-start | bytes 388
Sparse Core Ops, SparseCore 0:
  12.0 99.3 all-gather.4
  131.1 75.8 all-gather.6
  218.8 218.2 reduce-scatter.2
  440.1 81.1 all-gather.8
  536.2 217.1 reduce-scatter.4
  755.9 81.0 all-gather.10
where the time goes:
time: 853 us; the launch traced here: 852 us
  waiting for transfers between devices  643 us (75%)
  blocking collectives  92.9 us (11%)
  other arithmetic  37.4 us (4%)
  local copies, waits for them, and re-layouts  36.1 us (4%)
  matrix products  28.2 us (3%)
  between operations  14.3 us (2%)
    reduce_scatter x1, waiting for transfers between devices, body(): lax.psum_scatter(jnp.dot(row_block, output_weight, preferred_element_type...  218 us
    reduce_scatter x1, waiting for transfers between devices, body(): lax.psum_scatter(jnp.dot(hidden, down_weight, preferred_element_type=jnp....  142 us
    unnamed x2, blocking collectives  92.9 us
    all_gather x1, waiting for transfers between devices, body(): normed_ffn = lax.all_gather(normed_own, 'ctx', axis=0, tiled=True)  81.2 us
    all_gather x1, waiting for transfers between devices, body(): final_all = lax.all_gather(final_own, 'ctx', axis=0, tiled=True)  80.9 us
    all_gather x1, waiting for transfers between devices, body(): kv_all = lax.all_gather(kv_local, 'ctx', axis=0, tiled=True)  67.6 us
    all_gather x1, waiting for transfers between devices, body(): lax.all_gather(padded_rows, 'ctx', axis=0, tiled=True)  52.6 us
    gather x3, other arithmetic, body(): flat_row = source * MOST + rank_ids - run_starts[source]  19.9 us
  transfers between devices with their start and end apart: 6, of which 6 were waited for; matrix products, arithmetic and copies ran while one was open for 4% of the time, Pallas kernels for 0%

commit v1 on v0

v1 whole, which is shorter than its diff:
```python
import jax
import jax.numpy as jnp
from jax import lax
from jax.sharding import PartitionSpec as P

QUERY_HEADS = 32
KEY_VALUE_HEADS = 8
HEAD_SIZE = 128
PICK_DEV = 16
MOST = 32


norm_eps = 1e-05
rope_base = 500000.0


def rms_scale(matrix, gain_vec):
    mean_square = jnp.mean(matrix * matrix, axis=-1, keepdims=True)
    return matrix * lax.rsqrt(mean_square + norm_eps) * gain_vec


def apply_rotary(values, token_positions):
    half_dim = values.shape[-1] // 2
    frequency = rope_base ** (-(jnp.arange(half_dim, dtype=jnp.float32) * 2.0) / values.shape[-1])
    angles = token_positions.astype(jnp.float32)[:, None] * frequency[None, :]
    cosine = jnp.cos(angles)
    sine_part = jnp.sin(angles)
    lower_half = values[..., :half_dim]
    upper_half = values[..., half_dim:]
    return jnp.concatenate(
        (
            lower_half * cosine - upper_half * sine_part,
            upper_half * cosine + lower_half * sine_part,
        ),
        axis=-1,
    )


def reduce_scatter_rows(partial, ctx_size):
    rows, width = partial.shape
    pieces = lax.all_to_all(
        partial.reshape(ctx_size, rows // ctx_size, width), "ctx", 0, 0, tiled=True
    )
    return jnp.sum(pieces.astype(jnp.float32), axis=0)


def body(
    tokens,
    pick_flags,
    gate_scales,
    attn_gain,
    query_weight,
    key_weight,
    value_matrix,
    output_weight,
    ffn_gain,
    gate_weight,
    up_weight,
    down_weight,
):
    tok_local, width = tokens.shape
    ctx_size = lax.axis_size("ctx")
    my_index = lax.axis_index("ctx")
    picked_count = PICK_DEV * ctx_size
    half_pick = PICK_DEV // 2
    half_cycle = ctx_size // 2
    slot_of = jnp.cumsum(pick_flags) - 1
    token_ids = jnp.arange(tok_local, dtype=jnp.int32)
    slot_match = (jnp.arange(MOST, dtype=jnp.int32)[:, None] == slot_of[None, :]) & (
        pick_flags[None, :] == 1
    )
    chosen = jnp.sum(jnp.where(slot_match, token_ids[None, :], 0), axis=1)
    filled = jnp.any(slot_match, axis=1)
    local_index = jnp.where(filled, chosen, -1)
    padded_rows = jnp.where(filled[:, None], tokens[chosen], jnp.zeros((), jnp.bfloat16))
    padded_gate = jnp.where(filled, gate_scales[chosen], jnp.zeros((), jnp.bfloat16))
    lane = jnp.arange(128, dtype=jnp.int32)[None, :]
    extra = jnp.where(
        lane == 0,
        local_index.astype(jnp.bfloat16)[:, None],
        jnp.where(lane == 1, padded_gate[:, None], jnp.zeros((), jnp.bfloat16)),
    )
    packed = jnp.concatenate((padded_rows, extra), axis=1)
    all_packed = lax.all_gather(packed, "ctx", axis=0, tiled=True)
    all_rows = all_packed[:, :width]
    all_index = all_packed[:, width].astype(jnp.int32)
    all_gate = all_packed[:, width + 1]
    counts = jnp.sum((all_index >= 0).reshape(ctx_size, MOST).astype(jnp.int32), axis=1)
    run_ends = jnp.cumsum(counts)
    run_starts = run_ends - counts
    order_ids = jnp.arange(picked_count, dtype=jnp.int32)
    owner_of = order_ids // PICK_DEV
    within = order_ids % PICK_DEV
    low_part = within < half_pick
    rank_block = jnp.where(low_part, owner_of, (owner_of + half_cycle) % ctx_size)
    rank_inner = jnp.where(low_part, 2 * within, 2 * (within - half_pick) + 1)
    rank_ids = rank_block * PICK_DEV + rank_inner
    source = jnp.sum((run_ends[None, :] <= rank_ids[:, None]).astype(jnp.int32), axis=1)
    flat_row = source * MOST + rank_ids - run_starts[source]
    picked_rows = all_rows[flat_row]
    scales = all_gate[flat_row].astype(jnp.float32)
    token_positions = source * tok_local + all_index[flat_row]
    normalized_rows = rms_scale(picked_rows.astype(jnp.float32), attn_gain).astype(jnp.bfloat16)
    queries = jnp.dot(normalized_rows, query_weight, preferred_element_type=jnp.float32)
    queries = apply_rotary(queries, token_positions).astype(jnp.bfloat16)
    kv_weight = jnp.concatenate((key_weight, value_matrix), axis=1)
    kv_local = jnp.einsum(
        "pd,dc->cp", normalized_rows, kv_weight, preferred_element_type=jnp.float32
    ).astype(jnp.bfloat16)
    comps = key_weight.shape[1] // KEY_VALUE_HEADS
    query_group_width = QUERY_HEADS // KEY_VALUE_HEADS
    by_head = jnp.transpose(
        kv_local.reshape(2, comps, KEY_VALUE_HEADS, picked_count), (2, 0, 1, 3)
    )
    send = jnp.repeat(by_head, query_group_width, axis=0)
    got = lax.all_to_all(send, "ctx", 0, 0, tiled=True)
    key_cols = got[:, 0].reshape(ctx_size * comps, picked_count)
    value_cols = got[:, 1].reshape(ctx_size * comps, picked_count)
    keys_here = apply_rotary(key_cols.T.astype(jnp.float32), token_positions).astype(jnp.bfloat16)
    values_here = value_cols.T
    scores = jnp.dot(queries, keys_here.T, preferred_element_type=jnp.float32) / jnp.sqrt(
        jnp.float32(HEAD_SIZE)
    )
    allowed = token_positions[None, :] <= token_positions[:, None]
    scores = jnp.where(allowed, scores, -jnp.inf)
    row_max = jnp.max(scores, axis=1, keepdims=True)
    exp_terms = jnp.exp(scores - row_max)
    prob_bf = (exp_terms / jnp.sum(exp_terms, axis=1, keepdims=True)).astype(jnp.bfloat16)
    head_out = jnp.dot(prob_bf, values_here, preferred_element_type=jnp.float32).astype(jnp.bfloat16)
    own_start = my_index * PICK_DEV
    own_rows = lax.dynamic_slice_in_dim(picked_rows, own_start, PICK_DEV, 0).astype(jnp.float32)
    attn_own = reduce_scatter_rows(
        jnp.dot(head_out, output_weight, preferred_element_type=jnp.float32).astype(jnp.bfloat16),
        ctx_size,
    )
    mixed_own = own_rows + attn_own
    normed_own = rms_scale(mixed_own, ffn_gain).astype(jnp.bfloat16)
    normed_ffn = lax.all_gather(normed_own, "ctx", axis=0, tiled=True)
    gate_proj = jnp.dot(normed_ffn, gate_weight, preferred_element_type=jnp.float32)
    up_proj = jnp.dot(normed_ffn, up_weight, preferred_element_type=jnp.float32)
    hidden = (jax.nn.silu(gate_proj) * up_proj).astype(jnp.bfloat16)
    ffn_own = reduce_scatter_rows(
        jnp.dot(hidden, down_weight, preferred_element_type=jnp.float32).astype(jnp.bfloat16),
        ctx_size,
    )
    scale_own = lax.dynamic_slice_in_dim(scales, own_start, PICK_DEV, 0)
    final_own = (own_rows + scale_own[:, None] * (attn_own + ffn_own)).astype(jnp.bfloat16)
    final_all = lax.all_gather(final_own, "ctx", axis=0, tiled=True)
    my_start = run_starts[my_index]
    rank_here = jnp.clip(my_start + slot_of, 0, picked_count - 1)
    inner_here = rank_here % PICK_DEV
    odd_here = inner_here % 2
    owner_here = (rank_here // PICK_DEV + odd_here * half_cycle) % ctx_size
    take_rows = owner_here * PICK_DEV + inner_here // 2 + odd_here * half_pick
    return jnp.where(pick_flags[:, None] == 1, final_all[take_rows], tokens)


def solution(mesh):
    in_specs = (
        P(("dp", "ctx"), None),
        P(("dp", "ctx")),
        P(("dp", "ctx")),
        P(),
        P(None, "ctx"),
        P(None, "ctx"),
        P(None, "ctx"),
        P("ctx", None),
        P(),
        P(None, "ctx"),
        P(None, "ctx"),
        P("ctx", None),
    )
    out_specs = P(("dp", "ctx"), None)
    return jax.shard_map(body, mesh=mesh, in_specs=in_specs, out_specs=out_specs, check_vma=False)
```

time: 853 us -> 594 us (0.70)
  waiting for transfers between devices: 643 us -> 447 us
  blocking collectives: 92.9 us -> 0 us
  starting transfers between devices: 0.61 us -> 18.5 us
    reduce_scatter x2 -> x0, waiting for transfers between devices: 360 us -> none  [the longest x1 218 us: body(): lax.psum_scatter(jnp.dot(row_block, output_weight, preferred_element_type...]
    all_to_all x0 -> x3, waiting for transfers between devices: none -> 188 us  [the longest x2 181 us: reduce_scatter_rows(): lax.all_to_all(partial.reshape(ctx_size, rows // ctx_size, width), 'ctx',...]
    unnamed x2 -> x0, blocking collectives: 92.9 us -> none
    all_gather x2 -> x1, waiting for transfers between devices: 120 us -> 101 us  [body(): all_packed = lax.all_gather(packed, 'ctx', axis=0, tiled=True)]
    all_to_all x0 -> x3, starting transfers between devices: none -> 18.2 us  [the longest x2 10.6 us: reduce_scatter_rows(): lax.all_to_all(partial.reshape(ctx_size, rows // ctx_size, width), 'ctx',...]
  transfers between devices with their start and end apart: 6 -> 6, of which waited for: 6 -> 6; matrix products, arithmetic and copies ran while one was open for 4% -> 2% of each run, Pallas kernels for 0% -> 0%
where the time goes in v1:
time: 594 us; the launch traced here: 593 us
  waiting for transfers between devices  447 us (75%)
  other arithmetic  43.2 us (7%)
  local copies, waits for them, and re-layouts  42.8 us (7%)
  matrix products  27.6 us (5%)
  starting transfers between devices  18.5 us (3%)
  between operations  13.4 us (2%)
    all_to_all x2, waiting for transfers between devices, reduce_scatter_rows(): lax.all_to_all(partial.reshape(ctx_size, rows // ctx_size, width), 'ctx',...  181 us
    all_gather x1, waiting for transfers between devices, body(): all_packed = lax.all_gather(packed, 'ctx', axis=0, tiled=True)  101 us
    all_gather x1, waiting for transfers between devices, body(): normed_ffn = lax.all_gather(normed_own, 'ctx', axis=0, tiled=True)  79.8 us
    all_gather x1, waiting for transfers between devices, body(): final_all = lax.all_gather(final_own, 'ctx', axis=0, tiled=True)  78.3 us
    gather x3, other arithmetic, body(): flat_row = source * MOST + rank_ids - run_starts[source]  19.8 us
    gather x1, local copies, waits for them, and re-layouts, body(): picked_rows = all_rows[flat_row]  13 us
  transfers between devices with their start and end apart: 6, of which 6 were waited for; matrix products, arithmetic and copies ran while one was open for 2% of the time, Pallas kernels for 0%

profile of v1, /device:TPU:32, one launch (start us, length us, event | category | flops | bytes accessed | tf_op | source)
XLA Modules:
  0.0 592.9 jit_solution(4322541667487675454)
XLA Ops:
  13.4 100.8 %all-gather.4.cloned.1.call-done = bf16[1024,4224]{1,0:T(8,128)(2,1)} async-done(((bf16[32,4224]{1,0:T(8,128)(2,1)}), bf16[1024,4224]{1,0:T(8,128)(2,1)}) %all-gather.4.cloned.1.call-update) | async-done | bytes 8650768 | tf_op jit(solution)/shard_map/all_gather | solution.py:84
  117.5 4.4 compare_select_fusion.5
  122.0 15.2 %select_select_fusion.1 = s32[512]{0:T(512)S(1)} fusion(pred[512]{0:T(512)(128)(4,1)S(1)} %get-tuple-element.31, pred[512]{0:T(512)(128)(4,1)S(1)} %get-tuple-element.30, pred[512]{0:T(512)(128)(4,1)S(1)} %get-tuple-element.29, pred[512]{0:T(512)(128)(4,1)S(1)} %get-tuple-element.28, pred[512]{0:T(512)(128)(4,1)S(1)} %get-tuple-element.27, ...), kind=kLoop, calls=%fused_computation.170 | loop fusion | flops 12800 | bytes 16996 | tf_op jit(solution)/shard_map/gather | solution.py:99
  137.3 7.7 %slice.81 = bf16[1024,4096]{1,0:T(8,128)(2,1)} slice(bf16[1024,4224]{1,0:T(8,128)(2,1)} %all-gather.4.cloned.1.call-done), slice={[0:1024], [0:4096]} | slice | bytes 16777216 | tf_op jit(solution)/shard_map/slice | solution.py:85
  145.1 13.0 %gather_fusion.2 = bf16[512,4096]{1,0:T(8,128)(2,1)} fusion(bf16[1024,4096]{1,0:T(8,128)(2,1)} %slice.81, s32[1024]{0:T(1024)S(1)} %pad_clamp_fusion.1), kind=kCustom, calls=%fused_computation.2 | custom fusion | bytes 8390656 | tf_op jit(solution)/shard_map/gather | solution.py:100
  160.4 3.2 fusion
  163.8 2.5 fusion.9
  167.2 7.6 %all-to-all-start = ((bf16[32,2,4,512]{3,2,1,0:T(4,128)(2,1)}), bf16[32,2,4,512]{3,2,1,0:T(4,128)(2,1)S(1)}, u32[]{:S(2)}, u32[]{:S(2)}) async-start(bf16[32,2,4,512]{3,2,1,0:T(4,128)(2,1)} %bitcast.42), calls=%async_computation | async-start | bytes 524288 | tf_op jit(solution)/shard_map/all_to_all | solution.py:116
  174.8 4.8 fusion.7
  179.6 7.1 %all-to-all-done = bf16[32,2,4,512]{3,2,1,0:T(4,128)(2,1)S(1)} async-done(((bf16[32,2,4,512]{3,2,1,0:T(4,128)(2,1)}), bf16[32,2,4,512]{3,2,1,0:T(4,128)(2,1)S(1)}, u32[]{:S(2)}, u32[]{:S(2)}) %all-to-all-start) | async-done | bytes 262176 | tf_op jit(solution)/shard_map/all_to_all | solution.py:116
  191.5 5.1 convolution_convert_fusion
  196.7 4.7 all-to-all-start.1
  201.5 93.7 %all-to-all-done.1 = bf16[32,16,4096]{2,1,0:T(8,128)(2,1)} async-done(((bf16[32,16,4096]{2,1,0:T(8,128)(2,1)}), bf16[32,16,4096]{2,1,0:T(8,128)(2,1)}, u32[]{:S(2)}, u32[]{:S(2)}) %all-to-all-start.1) | async-done | bytes 4194336 | tf_op jit(solution)/shard_map/all_to_all | solution.py:41
  295.1 2.9 convert_reduce_fusion.1
  300.8 79.8 %all-gather.6.cloned.1.call-done = bf16[512,4096]{1,0:T(8,128)(2,1)} async-done(((bf16[16,4096]{1,0:T(8,128)(2,1)}), bf16[512,4096]{1,0:T(8,128)(2,1)}) %all-gather.6.cloned.1.call-update) | async-done | bytes 4194320 | tf_op jit(solution)/shard_map/all_gather | solution.py:138
  380.6 5.6 fusion.79
  386.2 9.2 %convolution_convert_fusion.1 = bf16[512,4096]{1,0:T(8,128)(2,1)} fusion(bf16[352,4096]{1,0:T(8,128)(2,1)S(1)} %copy-done, bf16[512,4096]{1,0:T(8,128)(2,1)} %all-gather.6.cloned.1.call-done, bf16[4096,352]{0,1:T(8,128)(2,1)} %param.22, f32[512,352]{0,1:T(8,128)} %fusion.79), kind=kOutput, calls=%fused_computation.14 | convolution fusion | flops 2955968512 | bytes 14876672 | tf_op jit(solution)/shard_map/dot_general | solution.py:143
  395.4 5.9 all-to-all-start.2
  402.7 3.5 gather_fusion.3
  406.3 87.7 %all-to-all-done.2 = bf16[32,16,4096]{2,1,0:T(8,128)(2,1)} async-done(((bf16[32,16,4096]{2,1,0:T(8,128)(2,1)}), bf16[32,16,4096]{2,1,0:T(8,128)(2,1)}, u32[]{:S(2)}, u32[]{:S(2)}) %all-to-all-start.2) | async-done | bytes 4194336 | tf_op jit(solution)/shard_map/all_to_all | solution.py:41
  494.0 2.8 convert_reduce_fusion
  499.5 78.3 %all-gather.8.cloned.1.call-done = bf16[512,4096]{1,0:T(8,128)(2,1)} async-done(((bf16[16,4096]{1,0:T(8,128)(2,1)}), bf16[512,4096]{1,0:T(8,128)(2,1)}) %all-gather.8.cloned.1.call-update) | async-done | bytes 4194320 | tf_op jit(solution)/shard_map/all_gather | solution.py:148
  577.8 5.9 gather_fusion.5
  583.7 2.7 broadcast_select_fusion
  (66 shorter events, 25.3 us)
Async XLA Ops:
  6.5 379.7 %copy-start = (bf16[352,4096]{1,0:T(8,128)(2,1)S(1)}, bf16[352,4096]{1,0:T(8,128)(2,1)}, u32[]{:S(2)}) copy-start(bf16[352,4096]{1,0:T(8,128)(2,1)} %param.23) | copy-start | bytes 8650756
  6.5 107.7 %all-gather.4.cloned.1.call-start = ((), (), s32[]{:S(2)}) async-start(), calls=%async_computation.3 | async-start | bytes 8921088 | tf_op jit(solution)/shard_map/all_gather | solution.py:84
  158.1 5.5 copy-start.4
  160.4 3.5 copy-start.1
  167.2 19.5 %all-to-all-start = ((bf16[32,2,4,512]{3,2,1,0:T(4,128)(2,1)}), bf16[32,2,4,512]{3,2,1,0:T(4,128)(2,1)S(1)}, u32[]{:S(2)}, u32[]{:S(2)}) async-start(bf16[32,2,4,512]{3,2,1,0:T(4,128)(2,1)} %bitcast.42), calls=%async_computation | async-start | bytes 524288 | tf_op jit(solution)/shard_map/all_to_all | solution.py:116
  190.4 1.0 copy-start.2
  196.7 98.5 %all-to-all-start.1 = ((bf16[32,16,4096]{2,1,0:T(8,128)(2,1)}), bf16[32,16,4096]{2,1,0:T(8,128)(2,1)}, u32[]{:S(2)}, u32[]{:S(2)}) async-start(bf16[32,16,4096]{2,1,0:T(8,128)(2,1)} %bitcast.58), calls=%async_computation.1 | async-start | bytes 8388608 | tf_op jit(solution)/shard_map/all_to_all | solution.py:41
  201.4 97.7 %copy-start.3 = (f32[4096]{0:T(1024)S(1)}, f32[4096]{0:T(1024)}, u32[]{:S(2)}) copy-start(f32[4096]{0:T(1024)} %param.20) | copy-start | bytes 49156
  201.4 179.2 %all-gather.6.cloned.1.call-start = ((), (), s32[]{:S(2)}) async-start(), calls=%async_computation.4 | async-start | bytes 4325376 | tf_op jit(solution)/shard_map/all_gather | solution.py:138
  395.4 98.7 %all-to-all-start.2 = ((bf16[32,16,4096]{2,1,0:T(8,128)(2,1)}), bf16[32,16,4096]{2,1,0:T(8,128)(2,1)}, u32[]{:S(2)}, u32[]{:S(2)}) async-start(bf16[32,16,4096]{2,1,0:T(8,128)(2,1)} %bitcast.59), calls=%async_computation.2 | async-start | bytes 8388608 | tf_op jit(solution)/shard_map/all_to_all | solution.py:41
  401.3 176.5 %all-gather.8.cloned.1.call-start = ((), (), s32[]{:S(2)}) async-start(), calls=%async_computation.5 | async-start | bytes 4325376 | tf_op jit(solution)/shard_map/all_gather | solution.py:148
Sparse Core Ops, SparseCore 0:
  13.5 100.7 all-gather.3
  300.9 79.6 all-gather.5
  498.7 79.0 all-gather.7

commit v2 on v1

--- a/solution.py
+++ b/solution.py
@@ -62,6 +62,7 @@
     ctx_size = lax.axis_size("ctx")
     my_index = lax.axis_index("ctx")
     picked_count = PICK_DEV * ctx_size
+    slots = MOST * ctx_size
     half_pick = PICK_DEV // 2
     half_cycle = ctx_size // 2
     slot_of = jnp.cumsum(pick_flags) - 1
@@ -82,12 +83,41 @@
     )
     packed = jnp.concatenate((padded_rows, extra), axis=1)
     all_packed = lax.all_gather(packed, "ctx", axis=0, tiled=True)
-    all_rows = all_packed[:, :width]
     all_index = all_packed[:, width].astype(jnp.int32)
-    all_gate = all_packed[:, width + 1]
-    counts = jnp.sum((all_index >= 0).reshape(ctx_size, MOST).astype(jnp.int32), axis=1)
+    slot_filled = all_index >= 0
+    counts = jnp.sum(slot_filled.reshape(ctx_size, MOST).astype(jnp.int32), axis=1)
     run_ends = jnp.cumsum(counts)
     run_starts = run_ends - counts
+    slot_ids = jnp.arange(slots, dtype=jnp.int32)
+    slot_pos = (slot_ids // MOST) * tok_local + all_index
+    rope_pos = jnp.where(slot_filled, slot_pos, 0)
+    never = jnp.int32(1 << 30)
+    mask_pos = jnp.where(slot_filled, slot_pos, never)
+    normalized = rms_scale(all_packed[:, :width].astype(jnp.float32), attn_gain).astype(jnp.bfloat16)
+    queries = jnp.dot(normalized, query_weight, preferred_element_type=jnp.float32)
+    queries = apply_rotary(queries, rope_pos).astype(jnp.bfloat16)
+    kv_weight = jnp.concatenate((key_weight, value_matrix), axis=1)
+    kv_local = jnp.einsum(
+        "pd,dc->cp", normalized, kv_weight, preferred_element_type=jnp.float32
+    ).astype(jnp.bfloat16)
+    comps = key_weight.shape[1] // KEY_VALUE_HEADS
+    query_group_width = QUERY_HEADS // KEY_VALUE_HEADS
+    by_head = jnp.transpose(kv_local.reshape(2, comps, KEY_VALUE_HEADS, slots), (2, 0, 1, 3))
+    send = jnp.repeat(by_head, query_group_width, axis=0)
+    got = lax.all_to_all(send, "ctx", 0, 0, tiled=True)
+    key_cols = got[:, 0].reshape(ctx_size * comps, slots)
+    value_cols = got[:, 1].reshape(ctx_size * comps, slots)
+    keys_here = apply_rotary(key_cols.T.astype(jnp.float32), rope_pos).astype(jnp.bfloat16)
+    values_here = value_cols.T
+    scores = jnp.dot(queries, keys_here.T, preferred_element_type=jnp.float32) / jnp.sqrt(
+        jnp.float32(HEAD_SIZE)
+    )
+    allowed = mask_pos[None, :] <= mask_pos[:, None]
+    scores = jnp.where(allowed, scores, -jnp.inf)
+    row_max = jnp.max(scores, axis=1, keepdims=True)
+    exp_terms = jnp.exp(scores - row_max)
+    prob_bf = (exp_terms / jnp.sum(exp_terms, axis=1, keepdims=True)).astype(jnp.bfloat16)
+    head_pad = jnp.dot(prob_bf, values_here, preferred_element_type=jnp.float32).astype(jnp.bfloat16)
     order_ids = jnp.arange(picked_count, dtype=jnp.int32)
     owner_of = order_ids // PICK_DEV
     within = order_ids % PICK_DEV
@@ -95,40 +125,16 @@
     rank_block = jnp.where(low_part, owner_of, (owner_of + half_cycle) % ctx_size)
     rank_inner = jnp.where(low_part, 2 * within, 2 * (within - half_pick) + 1)
     rank_ids = rank_block * PICK_DEV + rank_inner
-    source = jnp.sum((run_ends[None, :] <= rank_ids[:, None]).astype(jnp.int32), axis=1)
-    flat_row = source * MOST + rank_ids - run_starts[source]
-    picked_rows = all_rows[flat_row]
-    scales = all_gate[flat_row].astype(jnp.float32)
-    token_positions = source * tok_local + all_index[flat_row]
-    normalized_rows = rms_scale(picked_rows.astype(jnp.float32), attn_gain).astype(jnp.bfloat16)
-    queries = jnp.dot(normalized_rows, query_weight, preferred_element_type=jnp.float32)
-    queries = apply_rotary(queries, token_positions).astype(jnp.bfloat16)
-    kv_weight = jnp.concatenate((key_weight, value_matrix), axis=1)
-    kv_local = jnp.einsum(
-        "pd,dc->cp", normalized_rows, kv_weight, preferred_element_type=jnp.float32
-    ).astype(jnp.bfloat16)
-    comps = key_weight.shape[1] // KEY_VALUE_HEADS
-    query_group_width = QUERY_HEADS // KEY_VALUE_HEADS
-    by_head = jnp.transpose(
-        kv_local.reshape(2, comps, KEY_VALUE_HEADS, picked_count), (2, 0, 1, 3)
-    )
-    send = jnp.repeat(by_head, query_group_width, axis=0)
-    got = lax.all_to_all(send, "ctx", 0, 0, tiled=True)
-    key_cols = got[:, 0].reshape(ctx_size * comps, picked_count)
-    value_cols = got[:, 1].reshape(ctx_size * comps, picked_count)
-    keys_here = apply_rotary(key_cols.T.astype(jnp.float32), token_positions).astype(jnp.bfloat16)
-    values_here = value_cols.T
-    scores = jnp.dot(queries, keys_here.T, preferred_element_type=jnp.float32) / jnp.sqrt(
-        jnp.float32(HEAD_SIZE)
-    )
-    allowed = token_positions[None, :] <= token_positions[:, None]
-    scores = jnp.where(allowed, scores, -jnp.inf)
-    row_max = jnp.max(scores, axis=1, keepdims=True)
-    exp_terms = jnp.exp(scores - row_max)
-    prob_bf = (exp_terms / jnp.sum(exp_terms, axis=1, keepdims=True)).astype(jnp.bfloat16)
-    head_out = jnp.dot(prob_bf, values_here, preferred_element_type=jnp.float32).astype(jnp.bfloat16)
+    before = (run_ends[None, :] <= rank_ids[:, None]).astype(jnp.int32)
+    source = jnp.sum(before, axis=1)
+    flat_row = rank_ids + jnp.sum(before * (MOST - counts)[None, :], axis=1)
+    pick_onehot = (flat_row[:, None] == slot_ids[None, :]).astype(jnp.bfloat16)
+    head_out = jnp.dot(pick_onehot, head_pad, preferred_element_type=jnp.float32).astype(jnp.bfloat16)
     own_start = my_index * PICK_DEV
-    own_rows = lax.dynamic_slice_in_dim(picked_rows, own_start, PICK_DEV, 0).astype(jnp.float32)
+    own_flat = lax.dynamic_slice_in_dim(flat_row, own_start, PICK_DEV, 0)
+    own_packed = all_packed[own_flat]
+    own_rows = own_packed[:, :width].astype(jnp.float32)
+    scale_own = own_packed[:, width + 1].astype(jnp.float32)
     attn_own = reduce_scatter_rows(
         jnp.dot(head_out, output_weight, preferred_element_type=jnp.float32).astype(jnp.bfloat16),
         ctx_size,
@@ -143,16 +149,25 @@
         jnp.dot(hidden, down_weight, preferred_element_type=jnp.float32).astype(jnp.bfloat16),
         ctx_size,
     )
-    scale_own = lax.dynamic_slice_in_dim(scales, own_start, PICK_DEV, 0)
     final_own = (own_rows + scale_own[:, None] * (attn_own + ffn_own)).astype(jnp.bfloat16)
-    final_all = lax.all_gather(final_own, "ctx", axis=0, tiled=True)
+    own_source = lax.dynamic_slice_in_dim(source, own_start, PICK_DEV, 0)
+    targets = jnp.arange(ctx_size, dtype=jnp.int32)[:, None]
+    first_half = (own_source[None, :half_pick] == targets)[:, :, None]
+    second_half = (own_source[None, half_pick:] == targets)[:, :, None]
+    zero = jnp.zeros((), jnp.bfloat16)
+    back = jnp.where(
+        first_half,
+        final_own[None, :half_pick],
+        jnp.where(second_half, final_own[None, half_pick:], zero),
+    )
+    returned = lax.all_to_all(back, "ctx", 0, 0, tiled=True).reshape(ctx_size * half_pick, width)
     my_start = run_starts[my_index]
     rank_here = jnp.clip(my_start + slot_of, 0, picked_count - 1)
     inner_here = rank_here % PICK_DEV
     odd_here = inner_here % 2
     owner_here = (rank_here // PICK_DEV + odd_here * half_cycle) % ctx_size
-    take_rows = owner_here * PICK_DEV + inner_here // 2 + odd_here * half_pick
-    return jnp.where(pick_flags[:, None] == 1, final_all[take_rows], tokens)
+    take_rows = owner_here * half_pick + inner_here // 2
+    return jnp.where(pick_flags[:, None] == 1, returned[take_rows], tokens)
 
 
 def solution(mesh):

time: 594 us -> 541 us (0.911)
  waiting for transfers between devices: 447 us -> 418 us
  local copies, waits for them, and re-layouts: 42.8 us -> 19.9 us
  other arithmetic: 43.2 us -> 26.9 us
  matrix products: 27.6 us -> 35.9 us
  starting transfers between devices: 18.5 us -> 25.1 us
    all_gather x1 -> x0, waiting for transfers between devices: 78.3 us -> none  [body(): final_all = lax.all_gather(final_own, 'ctx', axis=0, tiled=True)]
    all_to_all x0 -> x1, waiting for transfers between devices: none -> 47.2 us  [body(): lax.all_to_all(back, 'ctx', 0, 0, tiled=True)]
    gather x5 -> x2, other arithmetic: 19.8 us -> 0.02 us  [the longest x1 0.01 us: body(): own_packed = all_packed[own_flat]]
    gather x5 -> x2, local copies, waits for them, and re-layouts: 25.4 us -> 10.4 us  [the longest x1 5.33 us: body(): own_packed = all_packed[own_flat]]
    slice x2, local copies, waits for them, and re-layouts: 8.92 us -> 0.08 us  [the longest x1 0.07 us: body(): first_half = (own_source[None, :half_pick] == targets)[:, :, None]]
    dot_general x2 -> x3, matrix products: 7.29 us -> 15.1 us  [the longest x1 7.25 us: body(): jnp.dot(normalized, query_weight, preferred_element_type=jnp.float32)]
    all_to_all x0 -> x1, starting transfers between devices: none -> 6.44 us  [body(): lax.all_to_all(back, 'ctx', 0, 0, tiled=True)]
  transfers between devices with their start and end apart: 6 -> 6, of which waited for: 6 -> 6; matrix products, arithmetic and copies ran while one was open for 2% -> 3% of each run, Pallas kernels for 0% -> 0%
where the time goes in v2:
time: 541 us; the launch traced here: 540 us
  waiting for transfers between devices  418 us (77%)
  matrix products  35.9 us (7%)
  other arithmetic  26.9 us (5%)
  starting transfers between devices  25.1 us (5%)
  local copies, waits for them, and re-layouts  19.9 us (4%)
  between operations  13.7 us (3%)
    all_to_all x2, waiting for transfers between devices, reduce_scatter_rows(): lax.all_to_all(partial.reshape(ctx_size, rows // ctx_size, width), 'ctx',...  182 us
    all_gather x1, waiting for transfers between devices, body(): all_packed = lax.all_gather(packed, 'ctx', axis=0, tiled=True)  101 us
    all_gather x1, waiting for transfers between devices, body(): normed_ffn = lax.all_gather(normed_own, 'ctx', axis=0, tiled=True)  79.9 us
    all_to_all x1, waiting for transfers between devices, body(): lax.all_to_all(back, 'ctx', 0, 0, tiled=True)  47.2 us
  transfers between devices with their start and end apart: 6, of which 6 were waited for; matrix products, arithmetic and copies ran while one was open for 3% of the time, Pallas kernels for 0%

profile of v2, /device:TPU:32, one launch (start us, length us, event | category | flops | bytes accessed | tf_op | source)
XLA Modules:
  0.0 539.7 jit_solution(12251853546995794627)
XLA Ops:
  10.1 2.3 gather_fusion
  13.4 100.8 %all-gather.3.cloned.1.call-done = bf16[1024,4224]{1,0:T(8,128)(2,1)} async-done(((bf16[32,4224]{1,0:T(8,128)(2,1)}), bf16[1024,4224]{1,0:T(8,128)(2,1)}) %all-gather.3.cloned.1.call-update) | async-done | bytes 8650768 | tf_op jit(solution)/shard_map/all_gather | solution.py:85
  114.2 5.1 fusion
  121.4 6.2 %fusion.13 = bf16[64,1024]{1,0:T(8,128)(2,1)S(1)} fusion(f32[4096]{0:T(1024)S(1)} %copy-done.4, f32[1024]{0:T(1024)S(1)} %add_rsqrt_fusion, bf16[1024,4224]{1,0:T(8,128)(2,1)} %all-gather.3.cloned.1.call-done, bf16[4096,32]{0,1:T(8,128)(2,1)S(1)} %copy-done.3, bf16[4096,32]{0,1:T(8,128)(2,1)} %param.17), kind=kOutput, calls=%fused_computation.27 | convolution fusion | flops 554762240 | bytes 9064448 | tf_op jit(solution)/shard_map/pd,dc->cp/dot_general | solution.py:100
  128.7 7.6 %all-to-all-start = ((bf16[32,2,4,1024]{3,2,1,0:T(4,128)(2,1)}), bf16[32,2,4,1024]{3,2,1,0:T(4,128)(2,1)S(1)}, u32[]{:S(2)}, u32[]{:S(2)}) async-start(bf16[32,2,4,1024]{3,2,1,0:T(4,128)(2,1)} %bitcast.6), calls=%async_computation | async-start | bytes 1048576 | tf_op jit(solution)/shard_map/all_to_all | solution.py:107
  137.6 7.2 %fusion.9 = f32[1024,128]{0,1:T(8,128)} fusion(bf16[4096,128]{1,0:T(8,128)(2,1)} %param.16, f32[4096]{0:T(1024)S(1)} %copy-done.4, f32[1024]{0:T(1024)S(1)} %add_rsqrt_fusion, bf16[1024,4224]{1,0:T(8,128)(2,1)} %all-gather.3.cloned.1.call-done), kind=kOutput, calls=%fused_computation.23 | convolution fusion | flops 1090519040 | bytes 9981952 | tf_op jit(solution)/shard_map/dot_general | solution.py:97
  144.9 8.7 %all-to-all-done = bf16[32,2,4,1024]{3,2,1,0:T(4,128)(2,1)S(1)} async-done(((bf16[32,2,4,1024]{3,2,1,0:T(4,128)(2,1)}), bf16[32,2,4,1024]{3,2,1,0:T(4,128)(2,1)S(1)}, u32[]{:S(2)}, u32[]{:S(2)}) %all-to-all-start) | async-done | bytes 524320 | tf_op jit(solution)/shard_map/all_to_all | solution.py:107
  155.9 1.7 reshape_squeeze.4
  157.6 2.2 fusion.41
  163.3 5.2 convolution_convert_fusion
  168.5 4.9 all-to-all-start.1
  173.8 5.3 gather_fusion.2
  179.1 89.2 %all-to-all-done.1 = bf16[32,16,4096]{2,1,0:T(8,128)(2,1)} async-done(((bf16[32,16,4096]{2,1,0:T(8,128)(2,1)}), bf16[32,16,4096]{2,1,0:T(8,128)(2,1)}, u32[]{:S(2)}, u32[]{:S(2)}) %all-to-all-start.1) | async-done | bytes 4194336 | tf_op jit(solution)/shard_map/all_to_all | solution.py:41
  268.4 2.8 convert_reduce_fusion.1
  272.2 79.9 %all-gather.5.cloned.1.call-done = bf16[512,4096]{1,0:T(8,128)(2,1)} async-done(((bf16[16,4096]{1,0:T(8,128)(2,1)}), bf16[512,4096]{1,0:T(8,128)(2,1)}) %all-gather.5.cloned.1.call-update) | async-done | bytes 4194320 | tf_op jit(solution)/shard_map/all_gather | solution.py:144
  352.0 5.6 %fusion.93 = f32[512,352]{0,1:T(8,128)} fusion(bf16[512,4096]{1,0:T(8,128)(2,1)} %all-gather.5.cloned.1.call-done, bf16[4096,352]{0,1:T(8,128)(2,1)} %param.21), kind=kOutput, calls=%fused_computation.175 | convolution fusion | flops 1476395008 | bytes 7798784 | tf_op jit(solution)/shard_map/dot_general | solution.py:145
  357.7 9.1 %convolution_convert_fusion.1 = bf16[512,4096]{1,0:T(8,128)(2,1)} fusion(bf16[352,4096]{1,0:T(8,128)(2,1)S(1)} %copy-done, bf16[512,4096]{1,0:T(8,128)(2,1)} %all-gather.5.cloned.1.call-done, bf16[4096,352]{0,1:T(8,128)(2,1)} %param.22, f32[512,352]{0,1:T(8,128)} %fusion.93), kind=kOutput, calls=%fused_computation.12 | convolution fusion | flops 2955968512 | bytes 14876672 | tf_op jit(solution)/shard_map/dot_general | solution.py:149
  366.8 5.9 %all-to-all-start.2 = ((bf16[32,16,4096]{2,1,0:T(8,128)(2,1)}), bf16[32,16,4096]{2,1,0:T(8,128)(2,1)}, u32[]{:S(2)}, u32[]{:S(2)}) async-start(bf16[32,16,4096]{2,1,0:T(8,128)(2,1)} %bitcast.25), calls=%async_computation.2 | async-start | bytes 8388608 | tf_op jit(solution)/shard_map/all_to_all | solution.py:41
  373.1 92.4 %all-to-all-done.2 = bf16[32,16,4096]{2,1,0:T(8,128)(2,1)} async-done(((bf16[32,16,4096]{2,1,0:T(8,128)(2,1)}), bf16[32,16,4096]{2,1,0:T(8,128)(2,1)}, u32[]{:S(2)}, u32[]{:S(2)}) %all-to-all-start.2) | async-done | bytes 4194336 | tf_op jit(solution)/shard_map/all_to_all | solution.py:41
  465.5 2.8 convert_reduce_fusion
  470.1 6.4 %all-to-all-start.3 = ((bf16[32,8,4096]{2,1,0:T(8,128)(2,1)}), bf16[32,8,4096]{2,1,0:T(8,128)(2,1)}, u32[]{:S(2)}, u32[]{:S(2)}) async-start(bf16[32,8,4096]{2,1,0:T(8,128)(2,1)} %select_select_fusion), calls=%async_computation.3 | async-start | bytes 4194304 | tf_op jit(solution)/shard_map/all_to_all | solution.py:163
  478.0 47.2 %all-to-all-done.3 = bf16[32,8,4096]{2,1,0:T(8,128)(2,1)} async-done(((bf16[32,8,4096]{2,1,0:T(8,128)(2,1)}), bf16[32,8,4096]{2,1,0:T(8,128)(2,1)}, u32[]{:S(2)}, u32[]{:S(2)}) %all-to-all-start.3) | async-done | bytes 2097184 | tf_op jit(solution)/shard_map/all_to_all | solution.py:163
  525.2 5.0 gather_fusion.3
  530.2 2.7 broadcast_select_fusion
  (66 shorter events, 19.5 us)
Async XLA Ops:
  6.5 351.1 %copy-start = (bf16[352,4096]{1,0:T(8,128)(2,1)S(1)}, bf16[352,4096]{1,0:T(8,128)(2,1)}, u32[]{:S(2)}) copy-start(bf16[352,4096]{1,0:T(8,128)(2,1)} %param.23) | copy-start | bytes 8650756
  6.5 107.7 %all-gather.3.cloned.1.call-start = ((), (), s32[]{:S(2)}) async-start(), calls=%async_computation.4 | async-start | bytes 8921088 | tf_op jit(solution)/shard_map/all_gather | solution.py:85
  13.4 108.0 %copy-start.3 = (bf16[4096,32]{0,1:T(8,128)(2,1)S(1)}, bf16[4096,32]{0,1:T(8,128)(2,1)}, u32[]{:S(2)}) copy-start(bf16[4096,32]{0,1:T(8,128)(2,1)} %param.18) | copy-start | bytes 786436
  13.4 108.0 %copy-start.4 = (f32[4096]{0:T(1024)S(1)}, f32[4096]{0:T(1024)}, u32[]{:S(2)}) copy-start(f32[4096]{0:T(1024)} %param.15) | copy-start | bytes 49156
  128.7 24.9 %all-to-all-start = ((bf16[32,2,4,1024]{3,2,1,0:T(4,128)(2,1)}), bf16[32,2,4,1024]{3,2,1,0:T(4,128)(2,1)S(1)}, u32[]{:S(2)}, u32[]{:S(2)}) async-start(bf16[32,2,4,1024]{3,2,1,0:T(4,128)(2,1)} %bitcast.6), calls=%async_computation | async-start | bytes 1048576 | tf_op jit(solution)/shard_map/all_to_all | solution.py:107
  159.8 1.9 copy-start.1
  168.5 99.9 %all-to-all-start.1 = ((bf16[32,16,4096]{2,1,0:T(8,128)(2,1)}), bf16[32,16,4096]{2,1,0:T(8,128)(2,1)}, u32[]{:S(2)}, u32[]{:S(2)}) async-start(bf16[32,16,4096]{2,1,0:T(8,128)(2,1)} %bitcast.24), calls=%async_computation.1 | async-start | bytes 8388608 | tf_op jit(solution)/shard_map/all_to_all | solution.py:41
  173.4 98.0 %copy-start.2 = (f32[4096]{0:T(1024)S(1)}, f32[4096]{0:T(1024)}, u32[]{:S(2)}) copy-start(f32[4096]{0:T(1024)} %param.20) | copy-start | bytes 49156
  173.4 178.6 %all-gather.5.cloned.1.call-start = ((), (), s32[]{:S(2)}) async-start(), calls=%async_computation.5 | async-start | bytes 4325376 | tf_op jit(solution)/shard_map/all_gather | solution.py:144
  366.8 98.7 %all-to-all-start.2 = ((bf16[32,16,4096]{2,1,0:T(8,128)(2,1)}), bf16[32,16,4096]{2,1,0:T(8,128)(2,1)}, u32[]{:S(2)}, u32[]{:S(2)}) async-start(bf16[32,16,4096]{2,1,0:T(8,128)(2,1)} %bitcast.25), calls=%async_computation.2 | async-start | bytes 8388608 | tf_op jit(solution)/shard_map/all_to_all | solution.py:41
  470.1 55.1 %all-to-all-start.3 = ((bf16[32,8,4096]{2,1,0:T(8,128)(2,1)}), bf16[32,8,4096]{2,1,0:T(8,128)(2,1)}, u32[]{:S(2)}, u32[]{:S(2)}) async-start(bf16[32,8,4096]{2,1,0:T(8,128)(2,1)} %select_select_fusion), calls=%async_computation.3 | async-start | bytes 4194304 | tf_op jit(solution)/shard_map/all_to_all | solution.py:163
Sparse Core Ops, SparseCore 0:
  13.5 100.7 all-gather.2
  272.3 79.7 all-gather.4

commit v3 on v2

--- a/solution.py
+++ b/solution.py
@@ -1,13 +1,15 @@
 import jax
 import jax.numpy as jnp
 from jax import lax
-from jax.sharding import PartitionSpec as P
+from jax.sharding import Mesh, PartitionSpec as P
 
 QUERY_HEADS = 32
 KEY_VALUE_HEADS = 8
 HEAD_SIZE = 128
 PICK_DEV = 16
 MOST = 32
+Z_RUN = 8
+GROUP = ("cy", "cz")
 
 
 norm_eps = 1e-05
@@ -36,12 +38,17 @@
     )
 
 
-def reduce_scatter_rows(partial, ctx_size):
+def reduce_scatter_rows(partial, y_size, z_size):
     rows, width = partial.shape
-    pieces = lax.all_to_all(
-        partial.reshape(ctx_size, rows // ctx_size, width), "ctx", 0, 0, tiled=True
-    )
-    return jnp.sum(pieces.astype(jnp.float32), axis=0)
+    blocks = partial.reshape(z_size, y_size, rows // (y_size * z_size), width)
+    over_y = lax.all_to_all(blocks, "cy", 1, 1, tiled=True)
+    part = jnp.sum(over_y.astype(jnp.float32), axis=1).astype(jnp.bfloat16)
+    over_z = lax.all_to_all(part, "cz", 0, 0, tiled=True)
+    return jnp.sum(over_z.astype(jnp.float32), axis=0)
+
+
+def gather_rows(x):
+    return lax.all_gather(lax.all_gather(x, "cy", axis=0, tiled=True), "cz", axis=0, tiled=True)
 
 
 def body(
@@ -59,8 +66,12 @@
     down_weight,
 ):
     tok_local, width = tokens.shape
-    ctx_size = lax.axis_size("ctx")
-    my_index = lax.axis_index("ctx")
+    y_size = lax.axis_size("cy")
+    z_size = lax.axis_size("cz")
+    ctx_size = y_size * z_size
+    my_index = lax.axis_index("cy") * z_size + lax.axis_index("cz")
+    blk = jnp.arange(ctx_size, dtype=jnp.int32)
+    block_dev = (blk % y_size) * z_size + blk // y_size
     picked_count = PICK_DEV * ctx_size
     slots = MOST * ctx_size
     half_pick = PICK_DEV // 2
@@ -82,14 +93,15 @@
         jnp.where(lane == 1, padded_gate[:, None], jnp.zeros((), jnp.bfloat16)),
     )
     packed = jnp.concatenate((padded_rows, extra), axis=1)
-    all_packed = lax.all_gather(packed, "ctx", axis=0, tiled=True)
+    all_packed = gather_rows(packed)
     all_index = all_packed[:, width].astype(jnp.int32)
     slot_filled = all_index >= 0
-    counts = jnp.sum(slot_filled.reshape(ctx_size, MOST).astype(jnp.int32), axis=1)
+    counts_blk = jnp.sum(slot_filled.reshape(ctx_size, MOST).astype(jnp.int32), axis=1)
+    counts = counts_blk.reshape(z_size, y_size).T.reshape(ctx_size)
     run_ends = jnp.cumsum(counts)
     run_starts = run_ends - counts
     slot_ids = jnp.arange(slots, dtype=jnp.int32)
-    slot_pos = (slot_ids // MOST) * tok_local + all_index
+    slot_pos = block_dev[slot_ids // MOST] * tok_local + all_index
     rope_pos = jnp.where(slot_filled, slot_pos, 0)
     never = jnp.int32(1 << 30)
     mask_pos = jnp.where(slot_filled, slot_pos, never)
@@ -104,7 +116,7 @@
     query_group_width = QUERY_HEADS // KEY_VALUE_HEADS
     by_head = jnp.transpose(kv_local.reshape(2, comps, KEY_VALUE_HEADS, slots), (2, 0, 1, 3))
     send = jnp.repeat(by_head, query_group_width, axis=0)
-    got = lax.all_to_all(send, "ctx", 0, 0, tiled=True)
+    got = lax.all_to_all(send, GROUP, 0, 0, tiled=True)
     key_cols = got[:, 0].reshape(ctx_size * comps, slots)
     value_cols = got[:, 1].reshape(ctx_size * comps, slots)
     keys_here = apply_rotary(key_cols.T.astype(jnp.float32), rope_pos).astype(jnp.bfloat16)
@@ -127,8 +139,10 @@
     rank_ids = rank_block * PICK_DEV + rank_inner
     before = (run_ends[None, :] <= rank_ids[:, None]).astype(jnp.int32)
     source = jnp.sum(before, axis=1)
-    flat_row = rank_ids + jnp.sum(before * (MOST - counts)[None, :], axis=1)
-    pick_onehot = (flat_row[:, None] == slot_ids[None, :]).astype(jnp.bfloat16)
+    offset = rank_ids - jnp.sum(before * counts[None, :], axis=1)
+    flat_row = ((source % z_size) * y_size + source // z_size) * MOST + offset
+    flat_blocked = flat_row.reshape(ctx_size, PICK_DEV)[block_dev].reshape(picked_count)
+    pick_onehot = (flat_blocked[:, None] == slot_ids[None, :]).astype(jnp.bfloat16)
     head_out = jnp.dot(pick_onehot, head_pad, preferred_element_type=jnp.float32).astype(jnp.bfloat16)
     own_start = my_index * PICK_DEV
     own_flat = lax.dynamic_slice_in_dim(flat_row, own_start, PICK_DEV, 0)
@@ -137,17 +151,19 @@
     scale_own = own_packed[:, width + 1].astype(jnp.float32)
     attn_own = reduce_scatter_rows(
         jnp.dot(head_out, output_weight, preferred_element_type=jnp.float32).astype(jnp.bfloat16),
-        ctx_size,
+        y_size,
+        z_size,
     )
     mixed_own = own_rows + attn_own
     normed_own = rms_scale(mixed_own, ffn_gain).astype(jnp.bfloat16)
-    normed_ffn = lax.all_gather(normed_own, "ctx", axis=0, tiled=True)
+    normed_ffn = gather_rows(normed_own)
     gate_proj = jnp.dot(normed_ffn, gate_weight, preferred_element_type=jnp.float32)
     up_proj = jnp.dot(normed_ffn, up_weight, preferred_element_type=jnp.float32)
     hidden = (jax.nn.silu(gate_proj) * up_proj).astype(jnp.bfloat16)
     ffn_own = reduce_scatter_rows(
         jnp.dot(hidden, down_weight, preferred_element_type=jnp.float32).astype(jnp.bfloat16),
-        ctx_size,
+        y_size,
+        z_size,
     )
     final_own = (own_rows + scale_own[:, None] * (attn_own + ffn_own)).astype(jnp.bfloat16)
     own_source = lax.dynamic_slice_in_dim(source, own_start, PICK_DEV, 0)
@@ -160,7 +176,7 @@
         final_own[None, :half_pick],
         jnp.where(second_half, final_own[None, half_pick:], zero),
     )
-    returned = lax.all_to_all(back, "ctx", 0, 0, tiled=True).reshape(ctx_size * half_pick, width)
+    returned = lax.all_to_all(back, GROUP, 0, 0, tiled=True).reshape(ctx_size * half_pick, width)
     my_start = run_starts[my_index]
     rank_here = jnp.clip(my_start + slot_of, 0, picked_count - 1)
     inner_here = rank_here % PICK_DEV
@@ -171,19 +187,23 @@
 
 
 def solution(mesh):
+    dp_size, ctx_size = mesh.devices.shape
+    z_size = Z_RUN if ctx_size % Z_RUN == 0 else ctx_size
+    split = Mesh(mesh.devices.reshape(dp_size, ctx_size // z_size, z_size), ("dp", "cy", "cz"))
+    rows = ("dp", "cy", "cz")
     in_specs = (
-        P(("dp", "ctx"), None),
-        P(("dp", "ctx")),
-        P(("dp", "ctx")),
+        P(rows, None),
+        P(rows),
+        P(rows),
         P(),
-        P(None, "ctx"),
-        P(None, "ctx"),
-        P(None, "ctx"),
-        P("ctx", None),
+        P(None, GROUP),
+        P(None, GROUP),
+        P(None, GROUP),
+        P(GROUP, None),
         P(),
-        P(None, "ctx"),
-        P(None, "ctx"),
-        P("ctx", None),
-    )
-    out_specs = P(("dp", "ctx"), None)
-    return jax.shard_map(body, mesh=mesh, in_specs=in_specs, out_specs=out_specs, check_vma=False)
+        P(None, GROUP),
+        P(None, GROUP),
+        P(GROUP, None),
+    )
+    out_specs = P(rows, None)
+    return jax.shard_map(body, mesh=split, in_specs=in_specs, out_specs=out_specs, check_vma=False)

time: 541 us -> 530 us (0.980)
  waiting for transfers between devices: 418 us -> 251 us
  blocking collectives: 0 us -> 117 us
  other arithmetic: 26.9 us -> 58.1 us
  local copies, waits for them, and re-layouts: 19.9 us -> 27.5 us
    all_to_all x4, waiting for transfers between devices: 238 us -> 102 us  [the longest x1 48.2 us: body(): lax.all_to_all(back, GROUP, 0, 0, tiled=True)]
    all_to_all x0 -> x2, blocking collectives: none -> 103 us  [reduce_scatter_rows(): over_y = lax.all_to_all(blocks, 'cy', 1, 1, tiled=True)]
    all_gather x2 -> x3, waiting for transfers between devices: 181 us -> 149 us  [the longest x2 119 us: gather_rows(): lax.all_gather(lax.all_gather(x, 'cy', axis=0, tiled=True), 'cz', axis=0,...]
    mul x0 -> x1, other arithmetic: none -> 15.4 us  [body(): slot_pos = block_dev[slot_ids // MOST] * tok_local + all_index]
    all_gather x0 -> x1, blocking collectives: none -> 13.5 us  [gather_rows(): lax.all_gather(x, 'cy', axis=0, tiled=True)]
    gather x0 -> x27, other arithmetic: none -> 9.38 us  [the longest x26 9.38 us: body(): slot_pos = block_dev[slot_ids // MOST] * tok_local + all_index]
    reduce_sum x3 -> x5, other arithmetic: 5.8 us -> 11.3 us  [the longest x2 8.44 us: reduce_scatter_rows(): part = jnp.sum(over_y.astype(jnp.float32), axis=1).astype(jnp.bfloat16)]
  transfers between devices with their start and end apart: 6 -> 7, of which waited for: 6 -> 7; matrix products, arithmetic and copies ran while one was open for 3% -> 8% of each run, Pallas kernels for 0% -> 0%
where the time goes in v3:
time: 530 us; the launch traced here: 528 us
  waiting for transfers between devices  251 us (47%)
  blocking collectives  117 us (22%)
  other arithmetic  58.1 us (11%)
  matrix products  34.9 us (7%)
  local copies, waits for them, and re-layouts  27.5 us (5%)
  starting transfers between devices  26.2 us (5%)
  between operations  13.4 us (3%)
    all_gather x2, waiting for transfers between devices, gather_rows(): lax.all_gather(lax.all_gather(x, 'cy', axis=0, tiled=True), 'cz', axis=0,...  119 us
    all_to_all x2, blocking collectives, reduce_scatter_rows(): over_y = lax.all_to_all(blocks, 'cy', 1, 1, tiled=True)  103 us
    all_to_all x1, waiting for transfers between devices, body(): lax.all_to_all(back, GROUP, 0, 0, tiled=True)  48.2 us
    all_to_all x2, waiting for transfers between devices, reduce_scatter_rows(): over_z = lax.all_to_all(part, 'cz', 0, 0, tiled=True)  45.9 us
    all_gather x1, waiting for transfers between devices, gather_rows(): lax.all_gather(x, 'cy', axis=0, tiled=True)  29.4 us
    mul x1, other arithmetic, body(): slot_pos = block_dev[slot_ids // MOST] * tok_local + all_index  15.4 us
    all_gather x1, blocking collectives, gather_rows(): lax.all_gather(x, 'cy', axis=0, tiled=True)  13.5 us
    all_to_all x2, starting transfers between devices, reduce_scatter_rows(): over_z = lax.all_to_all(part, 'cz', 0, 0, tiled=True)  11.1 us
  transfers between devices with their start and end apart: 7, of which 7 were waited for; matrix products, arithmetic and copies ran while one was open for 8% of the time, Pallas kernels for 0%

profile of v3, /device:TPU:32, one launch (start us, length us, event | category | flops | bytes accessed | tf_op | source)
XLA Modules:
  0.0 527.9 jit_solution(11144931826340381880)
XLA Ops:
  13.4 29.4 %all-gather.4.cloned.1.call-done = bf16[128,4224]{1,0:T(8,128)(2,1)} async-done(((bf16[32,4224]{1,0:T(8,128)(2,1)}), bf16[128,4224]{1,0:T(8,128)(2,1)}) %all-gather.4.cloned.1.call-update) | async-done | bytes 1081360 | tf_op jit(solution)/shard_map/all_gather | solution.py:51
  48.3 4.6 select_reduce_fusion
  53.6 15.4 %select_multiply_fusion = s32[1024]{0:T(1024)S(1)} fusion(pred[1024]{0:T(1024)(128)(4,1)S(1)} %fusion.56, pred[1024]{0:T(1024)(128)(4,1)S(1)} %fusion.57, pred[1024]{0:T(1024)(128)(4,1)S(1)} %fusion.80, pred[1024]{0:T(1024)(128)(4,1)S(1)} %fusion.79, pred[1024]{0:T(1024)(128)(4,1)S(1)} %fusion.78, pred[1024]{0:T(1024)(128)(4,1)S(1)} %fusion.77, ...), kind=kLoop, calls=%fused_computation.217 | loop fusion | flops 26624 | bytes 33892 | tf_op jit(solution)/shard_map/mul | solution.py:104
  69.8 70.2 %all-gather.6.cloned.1.call-done = bf16[1024,4224]{1,0:T(8,128)(2,1)} async-done(((bf16[128,4224]{1,0:T(8,128)(2,1)}), bf16[1024,4224]{1,0:T(8,128)(2,1)}) %all-gather.6.cloned.1.call-update) | async-done | bytes 8650768 | tf_op jit(solution)/shard_map/all_gather | solution.py:51
  142.0 5.1 fusion
  147.1 5.2 fusion.13
  153.4 9.2 %all-to-all-start = ((bf16[32,2,4,1024]{3,2,1,0:T(4,128)(2,1)}), bf16[32,2,4,1024]{3,2,1,0:T(4,128)(2,1)}, u32[]{:S(2)}, u32[]{:S(2)}) async-start(bf16[32,2,4,1024]{3,2,1,0:T(4,128)(2,1)} %bitcast.61), calls=%async_computation | async-start | bytes 1048576 | tf_op jit(solution)/shard_map/all_to_all | solution.py:119
  165.1 7.2 %fusion.9 = f32[1024,128]{0,1:T(8,128)} fusion(bf16[4096,128]{1,0:T(8,128)(2,1)} %param.16, f32[4096]{0:T(1024)} %param.15, f32[1024]{0:T(1024)S(1)} %add_rsqrt_fusion, bf16[1024,4224]{1,0:T(8,128)(2,1)} %all-gather.6.cloned.1.call-done), kind=kOutput, calls=%fused_computation.25 | convolution fusion | flops 1090519040 | bytes 9981952 | tf_op jit(solution)/shard_map/dot_general | solution.py:109
  172.3 8.1 %all-to-all-done = bf16[32,2,4,1024]{3,2,1,0:T(4,128)(2,1)} async-done(((bf16[32,2,4,1024]{3,2,1,0:T(4,128)(2,1)}), bf16[32,2,4,1024]{3,2,1,0:T(4,128)(2,1)}, u32[]{:S(2)}, u32[]{:S(2)}) %all-to-all-start) | async-done | bytes 524320 | tf_op jit(solution)/shard_map/all_to_all | solution.py:119
  191.1 5.3 convolution_convert_fusion
  198.8 50.4 %all_to_all.30 = bf16[8,4,16,4096]{3,2,0,1:T(8,128)(2,1)} all-to-all(bf16[8,4,16,4096]{3,2,0,1:T(8,128)(2,1)S(1)} %copy.38), channel_id=1, replica_groups=mesh['dp'=8,'cy'=4,'cz'=8] {'cy'}, dimensions={1} | all-to-all | bytes 8388608 | tf_op jit(solution)/shard_map/all_to_all | solution.py:44
  253.4 4.5 all-to-all-start.2
  258.0 5.3 %gather_fusion.2 = bf16[16,4224]{1,0:T(8,128)(2,1)S(1)} fusion(bf16[1024,4224]{1,0:T(8,128)(2,1)} %all-gather.6.cloned.1.call-done, s32[1024]{0:T(1024)S(1)} %pad_clamp_fusion.2), kind=kCustom, calls=%fused_computation.2 | custom fusion | bytes 270400 | tf_op jit(solution)/shard_map/gather | solution.py:149
  263.4 20.0 %all-to-all-done.2 = bf16[8,16,4096]{2,1,0:T(8,128)(2,1)} async-done(((bf16[8,16,4096]{2,1,0:T(8,128)(2,1)}), bf16[8,16,4096]{2,1,0:T(8,128)(2,1)}, u32[]{:S(2)}, u32[]{:S(2)}) %all-to-all-start.2) | async-done | bytes 1048608 | tf_op jit(solution)/shard_map/all_to_all | solution.py:46
  285.0 13.5 %all_gather.14 = bf16[64,4096]{1,0:T(8,128)(2,1)} all-gather(bf16[16,4096]{1,0:T(8,128)(2,1)S(1)} %multiply_convert_fusion), channel_id=1, replica_groups=mesh['dp'=8,'cy'=4,'cz'=8] {'cy'}, dimensions={0}, use_global_device_ids=true | all-gather | bytes 655360 | tf_op jit(solution)/shard_map/all_gather | solution.py:51
  298.6 49.1 %all-gather.8.cloned.1.call-done = bf16[512,4096]{1,0:T(8,128)(2,1)} async-done(((bf16[64,4096]{1,0:T(8,128)(2,1)}), bf16[512,4096]{1,0:T(8,128)(2,1)}) %all-gather.8.cloned.1.call-update) | async-done | bytes 4194320 | tf_op jit(solution)/shard_map/all_gather | solution.py:51
  347.7 5.6 %fusion.170 = f32[512,352]{0,1:T(8,128)} fusion(bf16[512,4096]{1,0:T(8,128)(2,1)} %all-gather.8.cloned.1.call-done, bf16[4096,352]{0,1:T(8,128)(2,1)} %param.21), kind=kOutput, calls=%fused_computation.286 | convolution fusion | flops 1476395008 | bytes 7798784 | tf_op jit(solution)/shard_map/dot_general | solution.py:160
  353.3 9.2 %convolution_convert_fusion.1 = bf16[512,4096]{1,0:T(8,128)(2,1)} fusion(bf16[352,4096]{1,0:T(8,128)(2,1)S(1)} %copy-done, bf16[512,4096]{1,0:T(8,128)(2,1)} %all-gather.8.cloned.1.call-done, bf16[4096,352]{0,1:T(8,128)(2,1)} %param.22, f32[512,352]{0,1:T(8,128)} %fusion.170), kind=kOutput, calls=%fused_computation.11 | convolution fusion | flops 2955968512 | bytes 14876672 | tf_op jit(solution)/shard_map/dot_general | solution.py:164
  364.9 53.0 %all_to_all.31 = bf16[8,4,16,4096]{3,2,0,1:T(8,128)(2,1)} all-to-all(bf16[8,4,16,4096]{3,2,0,1:T(8,128)(2,1)S(1)} %copy.39), channel_id=1, replica_groups=mesh['dp'=8,'cy'=4,'cz'=8] {'cy'}, dimensions={1} | all-to-all | bytes 8388608 | tf_op jit(solution)/shard_map/all_to_all | solution.py:44
  422.2 6.6 %all-to-all-start.4 = ((bf16[8,16,4096]{2,1,0:T(8,128)(2,1)}), bf16[8,16,4096]{2,1,0:T(8,128)(2,1)}, u32[]{:S(2)}, u32[]{:S(2)}) async-start(bf16[8,16,4096]{2,1,0:T(8,128)(2,1)} %reduce_sum.123), calls=%async_computation.4 | async-start | bytes 2097152 | tf_op jit(solution)/shard_map/all_to_all | solution.py:46
  429.1 25.9 %all-to-all-done.4 = bf16[8,16,4096]{2,1,0:T(8,128)(2,1)} async-done(((bf16[8,16,4096]{2,1,0:T(8,128)(2,1)}), bf16[8,16,4096]{2,1,0:T(8,128)(2,1)}, u32[]{:S(2)}, u32[]{:S(2)}) %all-to-all-start.4) | async-done | bytes 1048608 | tf_op jit(solution)/shard_map/all_to_all | solution.py:46
  458.1 5.9 %all-to-all-start.5 = ((bf16[32,8,4096]{2,1,0:T(8,128)(2,1)}), bf16[32,8,4096]{2,1,0:T(8,128)(2,1)}, u32[]{:S(2)}, u32[]{:S(2)}) async-start(bf16[32,8,4096]{2,1,0:T(8,128)(2,1)} %select_select_fusion), calls=%async_computation.5 | async-start | bytes 4194304 | tf_op jit(solution)/shard_map/all_to_all | solution.py:179
  465.5 48.2 %all-to-all-done.5 = bf16[32,8,4096]{2,1,0:T(8,128)(2,1)} async-done(((bf16[32,8,4096]{2,1,0:T(8,128)(2,1)}), bf16[32,8,4096]{2,1,0:T(8,128)(2,1)}, u32[]{:S(2)}, u32[]{:S(2)}) %all-to-all-start.5) | async-done | bytes 2097184 | tf_op jit(solution)/shard_map/all_to_all | solution.py:179
  513.7 5.0 gather_fusion.4
  (125 shorter events, 52.7 us)
Async XLA Ops:
  6.5 346.8 %copy-start = (bf16[352,4096]{1,0:T(8,128)(2,1)S(1)}, bf16[352,4096]{1,0:T(8,128)(2,1)}, u32[]{:S(2)}) copy-start(bf16[352,4096]{1,0:T(8,128)(2,1)} %param.23) | copy-start | bytes 8650756
  6.5 36.2 %all-gather.4.cloned.1.call-start = ((), (), s32[]{:S(2)}) async-start(), calls=%async_computation.6 | async-start | bytes 1351680 | tf_op jit(solution)/shard_map/all_gather | solution.py:51
  7.4 2.7 copy-start.4
  13.4 126.6 %all-gather.6.cloned.1.call-start = ((), (), s32[]{:S(2)}) async-start(), calls=%async_computation.7 | async-start | bytes 9732096 | tf_op jit(solution)/shard_map/all_gather | solution.py:51
  141.9 5.2 copy-start.6
  141.9 5.2 copy-start.7
  141.9 5.2 copy-start.8
  153.4 26.9 %all-to-all-start = ((bf16[32,2,4,1024]{3,2,1,0:T(4,128)(2,1)}), bf16[32,2,4,1024]{3,2,1,0:T(4,128)(2,1)}, u32[]{:S(2)}, u32[]{:S(2)}) async-start(bf16[32,2,4,1024]{3,2,1,0:T(4,128)(2,1)} %bitcast.61), calls=%async_computation | async-start | bytes 1048576 | tf_op jit(solution)/shard_map/all_to_all | solution.py:119
  165.0 20.3 %copy-start.3 = (f32[64]{0:T(128)S(1)}, f32[64]{0:T(128)}, u32[]{:S(2)}) copy-start(f32[64]{0:T(128)} %multiply_power_fusion) | copy-start | bytes 772
  187.5 1.9 copy-start.1
  249.2 35.7 %copy-start.2 = (f32[4096]{0:T(1024)S(1)}, f32[4096]{0:T(1024)}, u32[]{:S(2)}) copy-start(f32[4096]{0:T(1024)} %param.20) | copy-start | bytes 49156
  253.4 29.9 %all-to-all-start.2 = ((bf16[8,16,4096]{2,1,0:T(8,128)(2,1)}), bf16[8,16,4096]{2,1,0:T(8,128)(2,1)}, u32[]{:S(2)}, u32[]{:S(2)}) async-start(bf16[8,16,4096]{2,1,0:T(8,128)(2,1)} %reduce_sum.120), calls=%async_computation.2 | async-start | bytes 2097152 | tf_op jit(solution)/shard_map/all_to_all | solution.py:46
  257.9 89.8 %all-gather.8.cloned.1.call-start = ((), (), s32[]{:S(2)}) async-start(), calls=%async_computation.8 | async-start | bytes 4718592 | tf_op jit(solution)/shard_map/all_gather | solution.py:51
  422.2 32.8 %all-to-all-start.4 = ((bf16[8,16,4096]{2,1,0:T(8,128)(2,1)}), bf16[8,16,4096]{2,1,0:T(8,128)(2,1)}, u32[]{:S(2)}, u32[]{:S(2)}) async-start(bf16[8,16,4096]{2,1,0:T(8,128)(2,1)} %reduce_sum.123), calls=%async_computation.4 | async-start | bytes 2097152 | tf_op jit(solution)/shard_map/all_to_all | solution.py:46
  458.1 55.5 %all-to-all-start.5 = ((bf16[32,8,4096]{2,1,0:T(8,128)(2,1)}), bf16[32,8,4096]{2,1,0:T(8,128)(2,1)}, u32[]{:S(2)}, u32[]{:S(2)}) async-start(bf16[32,8,4096]{2,1,0:T(8,128)(2,1)} %select_select_fusion), calls=%async_computation.5 | async-start | bytes 4194304 | tf_op jit(solution)/shard_map/all_to_all | solution.py:179
  513.7 5.0 copy-start.5
Sparse Core Ops, SparseCore 0:
  13.5 29.2 all-gather.3
  44.6 95.3 all-gather.5
  298.7 48.9 all-gather.7

commit v4 on v3

--- a/solution.py
+++ b/solution.py
@@ -1,6 +1,10 @@
+import functools
+
 import jax
 import jax.numpy as jnp
 from jax import lax
+from jax.experimental import pallas as pl
+from jax.experimental.pallas import tpu as pltpu
 from jax.sharding import Mesh, PartitionSpec as P
 
 QUERY_HEADS = 32
@@ -38,13 +42,87 @@
     )
 
 
-def reduce_scatter_rows(partial, y_size, z_size):
+MESH_ID = pl.DeviceIdType.MESH
+
+
+def _zring_rs_kernel(n, x_ref, out_ref, recv, sendbuf, send_sem, recv_sem, credit):
+    me = lax.axis_index("cz")
+    right = lax.rem(me + 1, n)
+    left = lax.rem(me + n - 1, n)
+    half = x_ref.shape[2] // 2
+    dest = (right, left)
+    sender = (left, right)
+
+    barrier = pltpu.get_barrier_semaphore()
+    for neighbour in (left, right):
+        pl.semaphore_signal(barrier, inc=1, device_id={"cz": neighbour}, device_id_type=MESH_ID)
+    pl.semaphore_wait(barrier, 2)
+
+    for step in range(n - 1):
+        slot = step % 2
+        copies = []
+        for d in range(2):
+            if step == 0:
+                first = lax.rem(me + n - 1, n) if d == 0 else lax.rem(me + 1, n)
+                src = x_ref.at[first, :, pl.ds(d * half, half)]
+            else:
+                pl.semaphore_wait(credit.at[d], 1)
+                src = sendbuf.at[d, (step - 1) % 2]
+            copy = pltpu.make_async_remote_copy(
+                src_ref=src,
+                dst_ref=recv.at[d, slot],
+                send_sem=send_sem.at[d, slot],
+                recv_sem=recv_sem.at[d, slot],
+                device_id={"cz": dest[d]},
+                device_id_type=MESH_ID,
+            )
+            copy.start()
+            copies.append(copy)
+        for d in range(2):
+            copies[d].wait_recv()
+            if d == 0:
+                chunk = lax.rem(me + 2 * n - step - 2, n)
+            else:
+                chunk = lax.rem(me + step + 2, n)
+            total = recv[d, slot].astype(jnp.float32) + x_ref[chunk, :, pl.ds(d * half, half)].astype(
+                jnp.float32
+            )
+            if step == n - 2:
+                out_ref[:, pl.ds(d * half, half)] = total
+            else:
+                sendbuf[d, slot] = total.astype(sendbuf.dtype)
+            if step <= n - 3:
+                pl.semaphore_signal(credit.at[d], inc=1, device_id={"cz": sender[d]}, device_id_type=MESH_ID)
+        for d in range(2):
+            copies[d].wait_send()
+
+
+def zring_reduce_scatter(x, collective_id):
+    n, rows, cols = x.shape
+    half = cols // 2
+    return pl.pallas_call(
+        functools.partial(_zring_rs_kernel, n),
+        out_shape=jax.ShapeDtypeStruct((rows, cols), jnp.float32),
+        in_specs=[pl.BlockSpec(memory_space=pltpu.VMEM)],
+        out_specs=pl.BlockSpec(memory_space=pltpu.VMEM),
+        scratch_shapes=[
+            pltpu.VMEM((2, 2, rows, half), x.dtype),
+            pltpu.VMEM((2, 2, rows, half), x.dtype),
+            pltpu.SemaphoreType.DMA((2, 2)),
+            pltpu.SemaphoreType.DMA((2, 2)),
+            pltpu.SemaphoreType.REGULAR((2,)),
+        ],
+        compiler_params=pltpu.CompilerParams(collective_id=collective_id, has_side_effects=True),
+    )(x)
+
+
+def reduce_scatter_rows(partial, y_size, z_size, collective_id):
     rows, width = partial.shape
-    blocks = partial.reshape(z_size, y_size, rows // (y_size * z_size), width)
-    over_y = lax.all_to_all(blocks, "cy", 1, 1, tiled=True)
-    part = jnp.sum(over_y.astype(jnp.float32), axis=1).astype(jnp.bfloat16)
-    over_z = lax.all_to_all(part, "cz", 0, 0, tiled=True)
-    return jnp.sum(over_z.astype(jnp.float32), axis=0)
+    own = rows // (y_size * z_size)
+    over_z = zring_reduce_scatter(partial.reshape(z_size, y_size * own, width), collective_id)
+    part = over_z.astype(jnp.bfloat16).reshape(y_size, own, width)
+    over_y = lax.all_to_all(part, "cy", 0, 0, tiled=True)
+    return jnp.sum(over_y.astype(jnp.float32), axis=0)
 
 
 def gather_rows(x):
@@ -93,15 +171,14 @@
         jnp.where(lane == 1, padded_gate[:, None], jnp.zeros((), jnp.bfloat16)),
     )
     packed = jnp.concatenate((padded_rows, extra), axis=1)
-    all_packed = gather_rows(packed)
+    all_packed = lax.all_gather(packed, GROUP, axis=0, tiled=True)
     all_index = all_packed[:, width].astype(jnp.int32)
     slot_filled = all_index >= 0
-    counts_blk = jnp.sum(slot_filled.reshape(ctx_size, MOST).astype(jnp.int32), axis=1)
-    counts = counts_blk.reshape(z_size, y_size).T.reshape(ctx_size)
+    counts = jnp.sum(slot_filled.reshape(ctx_size, MOST).astype(jnp.int32), axis=1)
     run_ends = jnp.cumsum(counts)
     run_starts = run_ends - counts
     slot_ids = jnp.arange(slots, dtype=jnp.int32)
-    slot_pos = block_dev[slot_ids // MOST] * tok_local + all_index
+    slot_pos = (slot_ids // MOST) * tok_local + all_index
     rope_pos = jnp.where(slot_filled, slot_pos, 0)
     never = jnp.int32(1 << 30)
     mask_pos = jnp.where(slot_filled, slot_pos, never)
@@ -140,7 +217,7 @@
     before = (run_ends[None, :] <= rank_ids[:, None]).astype(jnp.int32)
     source = jnp.sum(before, axis=1)
     offset = rank_ids - jnp.sum(before * counts[None, :], axis=1)
-    flat_row = ((source % z_size) * y_size + source // z_size) * MOST + offset
+    flat_row = source * MOST + offset
     flat_blocked = flat_row.reshape(ctx_size, PICK_DEV)[block_dev].reshape(picked_count)
     pick_onehot = (flat_blocked[:, None] == slot_ids[None, :]).astype(jnp.bfloat16)
     head_out = jnp.dot(pick_onehot, head_pad, preferred_element_type=jnp.float32).astype(jnp.bfloat16)
@@ -153,6 +230,7 @@
         jnp.dot(head_out, output_weight, preferred_element_type=jnp.float32).astype(jnp.bfloat16),
         y_size,
         z_size,
+        0,
     )
     mixed_own = own_rows + attn_own
     normed_own = rms_scale(mixed_own, ffn_gain).astype(jnp.bfloat16)
@@ -164,6 +242,7 @@
         jnp.dot(hidden, down_weight, preferred_element_type=jnp.float32).astype(jnp.bfloat16),
         y_size,
         z_size,
+        1,
     )
     final_own = (own_rows + scale_own[:, None] * (attn_own + ffn_own)).astype(jnp.bfloat16)
     own_source = lax.dynamic_slice_in_dim(source, own_start, PICK_DEV, 0)

time: 530 us -> 475 us (0.90)
  Pallas kernels: 0 us -> 124 us
  blocking collectives: 117 us -> 13.5 us
  waiting for transfers between devices: 251 us -> 214 us
  other arithmetic: 58.1 us -> 27 us
  local copies, waits for them, and re-layouts: 27.5 us -> 20.7 us
    pallas_call x0 -> x2, Pallas kernels: none -> 124 us  [zring_reduce_scatter(): pl.pallas_call(functools.partial(_zring_rs_kernel, n), out_shape=jax.Shap...]
    all_to_all x2 -> x0, blocking collectives: 103 us -> none  [reduce_scatter_rows(): over_y = lax.all_to_all(blocks, 'cy', 1, 1, tiled=True)]
    all_gather x1, waiting for transfers between devices: 29.4 us -> 101 us  [body(): all_packed = lax.all_gather(packed, GROUP, axis=0, tiled=True)]
    all_gather x2 -> x1, waiting for transfers between devices: 119 us -> 53 us  [gather_rows(): lax.all_gather(lax.all_gather(x, 'cy', axis=0, tiled=True), 'cz', axis=0,...]
    all_to_all x2, waiting for transfers between devices: 45.9 us -> 11.3 us  [reduce_scatter_rows(): over_y = lax.all_to_all(part, 'cy', 0, 0, tiled=True)]
    mul x1 -> x0, other arithmetic: 15.4 us -> none  [body(): slot_pos = block_dev[slot_ids // MOST] * tok_local + all_index]
    gather x26 -> x0, other arithmetic: 9.38 us -> none  [body(): slot_pos = block_dev[slot_ids // MOST] * tok_local + all_index]
    reduce_sum x4 -> x2, other arithmetic: 11.2 us -> 2.27 us  [reduce_scatter_rows(): return jnp.sum(over_y.astype(jnp.float32), axis=0)]
  transfers between devices with their start and end apart: 7 -> 6, of which waited for: 7 -> 6; matrix products, arithmetic and copies ran while one was open for 8% -> 3% of each run, Pallas kernels for 0% -> 0%
where the time goes in v4:
time: 475 us; the launch traced here: 474 us
  waiting for transfers between devices  214 us (45%)
  Pallas kernels  124 us (26%)
  matrix products  35.9 us (8%)
  other arithmetic  27 us (6%)
  starting transfers between devices  24.6 us (5%)
  local copies, waits for them, and re-layouts  20.7 us (4%)
  between operations  13.7 us (3%)
  blocking collectives  13.5 us (3%)
    pallas_call x2, Pallas kernels, zring_reduce_scatter(): pl.pallas_call(functools.partial(_zring_rs_kernel, n), out_shape=jax.Shap...  124 us
    all_gather x1, waiting for transfers between devices, body(): all_packed = lax.all_gather(packed, GROUP, axis=0, tiled=True)  101 us
    all_gather x1, waiting for transfers between devices, gather_rows(): lax.all_gather(lax.all_gather(x, 'cy', axis=0, tiled=True), 'cz', axis=0,...  53 us
    all_to_all x1, waiting for transfers between devices, body(): lax.all_to_all(back, GROUP, 0, 0, tiled=True)  40.4 us
    all_gather x1, blocking collectives, gather_rows(): lax.all_gather(x, 'cy', axis=0, tiled=True)  13.5 us
    all_to_all x2, waiting for transfers between devices, reduce_scatter_rows(): over_y = lax.all_to_all(part, 'cy', 0, 0, tiled=True)  11.3 us
  transfers between devices with their start and end apart: 6, of which 6 were waited for; matrix products, arithmetic and copies ran while one was open for 3% of the time, Pallas kernels for 0%

profile of v4, /device:TPU:32, one launch (start us, length us, event | category | flops | bytes accessed | tf_op | source)
XLA Modules:
  0.0 473.7 jit_solution(2725104883529557994)
XLA Ops:
  10.1 2.3 gather_fusion
  13.4 100.8 %all-gather.3.cloned.1.call-done = bf16[1024,4224]{1,0:T(8,128)(2,1)} async-done(((bf16[32,4224]{1,0:T(8,128)(2,1)}), bf16[1024,4224]{1,0:T(8,128)(2,1)}) %all-gather.3.cloned.1.call-update) | async-done | bytes 8650768 | tf_op jit(solution)/shard_map/all_gather | solution.py:174
  114.2 5.1 %fusion = f32[1024]{0:T(1024)S(1)} fusion(bf16[1024,4224]{1,0:T(8,128)(2,1)} %all-gather.3.cloned.1.call-done), kind=kLoop, calls=%fused_computation.7 | loop fusion | flops 12581888 | bytes 8392704 | tf_op jit(solution)/shard_map/reduce_sum | solution.py:24
  122.2 6.2 %fusion.13 = bf16[64,1024]{1,0:T(8,128)(2,1)S(1)} fusion(f32[4096]{0:T(1024)S(1)} %copy-done.4, f32[1024]{0:T(1024)S(1)} %add_rsqrt_fusion, bf16[1024,4224]{1,0:T(8,128)(2,1)} %all-gather.3.cloned.1.call-done, bf16[4096,32]{0,1:T(8,128)(2,1)S(1)} %copy-done.3, bf16[4096,32]{0,1:T(8,128)(2,1)} %param.17), kind=kOutput, calls=%fused_computation.26 | convolution fusion | flops 554762240 | bytes 9064448 | tf_op jit(solution)/shard_map/pd,dc->cp/dot_general | solution.py:189
  129.6 7.6 %all-to-all-start = ((bf16[32,2,4,1024]{3,2,1,0:T(4,128)(2,1)}), bf16[32,2,4,1024]{3,2,1,0:T(4,128)(2,1)S(1)}, u32[]{:S(2)}, u32[]{:S(2)}) async-start(bf16[32,2,4,1024]{3,2,1,0:T(4,128)(2,1)} %bitcast.7), calls=%async_computation | async-start | bytes 1048576 | tf_op jit(solution)/shard_map/all_to_all | solution.py:196
  138.4 7.2 %fusion.9 = f32[1024,128]{0,1:T(8,128)} fusion(bf16[4096,128]{1,0:T(8,128)(2,1)} %param.16, f32[4096]{0:T(1024)S(1)} %copy-done.4, f32[1024]{0:T(1024)S(1)} %add_rsqrt_fusion, bf16[1024,4224]{1,0:T(8,128)(2,1)} %all-gather.3.cloned.1.call-done), kind=kOutput, calls=%fused_computation.22 | convolution fusion | flops 1090519040 | bytes 9981952 | tf_op jit(solution)/shard_map/dot_general | solution.py:186
  145.7 8.7 %all-to-all-done = bf16[32,2,4,1024]{3,2,1,0:T(4,128)(2,1)S(1)} async-done(((bf16[32,2,4,1024]{3,2,1,0:T(4,128)(2,1)}), bf16[32,2,4,1024]{3,2,1,0:T(4,128)(2,1)S(1)}, u32[]{:S(2)}, u32[]{:S(2)}) %all-to-all-start) | async-done | bytes 524320 | tf_op jit(solution)/shard_map/all_to_all | solution.py:196
  158.4 2.2 fusion.41
  164.1 5.3 %convolution_convert_fusion = bf16[512,4096]{1,0:T(8,128)(2,1)} fusion(bf16[128,4096]{1,0:T(8,128)(2,1)} %param.19, bf16[1024,128]{1,0:T(8,128)(2,1)S(1)} %fusion.12, s32[512]{0:T(512)S(1)} %eq.110), kind=kOutput, calls=%fused_computation.10 | convolution fusion | flops 673775616 | bytes 5507072 | tf_op jit(solution)/shard_map/dot_general | solution.py:230
  169.4 61.1 %shard_map.118 = f32[64,4096]{1,0:T(8,128)} custom-call(bf16[8,64,4096]{2,1,0:T(8,128)(2,1)} %bitcast.28), custom_call_target="tpu_custom_call" | custom-call | tf_op jit(solution)/shard_map/pallas_call | solution.py:103
  232.6 4.1 all-to-all-start.1
  237.1 5.3 %gather_fusion.2 = bf16[16,4224]{1,0:T(8,128)(2,1)S(1)} fusion(bf16[1024,4224]{1,0:T(8,128)(2,1)} %all-gather.3.cloned.1.call-done, s32[1024]{0:T(1024)S(1)} %pad_clamp_fusion.2), kind=kCustom, calls=%fused_computation.2 | custom fusion | bytes 270400 | tf_op jit(solution)/shard_map/gather | solution.py:226
  242.4 3.1 all-to-all-done.1
  247.0 13.5 %all_gather.10 = bf16[64,4096]{1,0:T(8,128)(2,1)} all-gather(bf16[16,4096]{1,0:T(8,128)(2,1)S(1)} %multiply_convert_fusion), channel_id=1, replica_groups=mesh['dp'=8,'cy'=4,'cz'=8] {'cy'}, dimensions={0}, use_global_device_ids=true | all-gather | bytes 655360 | tf_op jit(solution)/shard_map/all_gather | solution.py:129
  260.8 53.0 %all-gather.5.cloned.1.call-done = bf16[512,4096]{1,0:T(8,128)(2,1)} async-done(((bf16[64,4096]{1,0:T(8,128)(2,1)}), bf16[512,4096]{1,0:T(8,128)(2,1)}) %all-gather.5.cloned.1.call-update) | async-done | bytes 4194320 | tf_op jit(solution)/shard_map/all_gather | solution.py:129
  313.9 5.6 %fusion.104 = f32[512,352]{0,1:T(8,128)} fusion(bf16[512,4096]{1,0:T(8,128)(2,1)} %all-gather.5.cloned.1.call-done, bf16[4096,352]{0,1:T(8,128)(2,1)} %param.21), kind=kOutput, calls=%fused_computation.205 | convolution fusion | flops 1476395008 | bytes 7798784 | tf_op jit(solution)/shard_map/dot_general | solution.py:238
  319.5 9.2 %convolution_convert_fusion.1 = bf16[512,4096]{1,0:T(8,128)(2,1)} fusion(bf16[352,4096]{1,0:T(8,128)(2,1)S(1)} %copy-done, bf16[512,4096]{1,0:T(8,128)(2,1)} %all-gather.5.cloned.1.call-done, bf16[4096,352]{0,1:T(8,128)(2,1)} %param.22, f32[512,352]{0,1:T(8,128)} %fusion.104), kind=kOutput, calls=%fused_computation.11 | convolution fusion | flops 2955968512 | bytes 14876672 | tf_op jit(solution)/shard_map/dot_general | solution.py:242
  328.7 62.7 %shard_map.119 = f32[64,4096]{1,0:T(8,128)} custom-call(bf16[8,64,4096]{2,1,0:T(8,128)(2,1)} %bitcast.29), custom_call_target="tpu_custom_call" | custom-call | tf_op jit(solution)/shard_map/pallas_call | solution.py:103
  393.5 4.3 all-to-all-start.2
  397.8 8.2 %all-to-all-done.2 = bf16[4,16,4096]{2,1,0:T(8,128)(2,1)} async-done(((bf16[4,16,4096]{2,1,0:T(8,128)(2,1)}), bf16[4,16,4096]{2,1,0:T(8,128)(2,1)}, u32[]{:S(2)}, u32[]{:S(2)}) %all-to-all-start.2) | async-done | bytes 524320 | tf_op jit(solution)/shard_map/all_to_all | solution.py:124
  408.9 8.3 %all-to-all-start.3 = ((bf16[32,8,4096]{2,1,0:T(8,128)(2,1)}), bf16[32,8,4096]{2,1,0:T(8,128)(2,1)}, u32[]{:S(2)}, u32[]{:S(2)}) async-start(bf16[32,8,4096]{2,1,0:T(8,128)(2,1)} %select_select_fusion), calls=%async_computation.3 | async-start | bytes 4194304 | tf_op jit(solution)/shard_map/all_to_all | solution.py:258
  418.7 40.4 %all-to-all-done.3 = bf16[32,8,4096]{2,1,0:T(8,128)(2,1)} async-done(((bf16[32,8,4096]{2,1,0:T(8,128)(2,1)}), bf16[32,8,4096]{2,1,0:T(8,128)(2,1)}, u32[]{:S(2)}, u32[]{:S(2)}) %all-to-all-start.3) | async-done | bytes 2097184 | tf_op jit(solution)/shard_map/all_to_all | solution.py:258
  459.1 5.0 %gather_fusion.4 = bf16[128,4096]{1,0:T(8,128)(2,1)} fusion(bf16[256,4096]{1,0:T(8,128)(2,1)} %bitcast.13, s32[1024]{0:T(1024)S(1)} %pad_clamp_fusion), kind=kCustom, calls=%fused_computation.4 | custom fusion | bytes 2097664 | tf_op jit(solution)/shard_map/gather | solution.py:265
  464.2 2.7 broadcast_select_fusion
  (78 shorter events, 27.8 us)
Async XLA Ops:
  6.5 313.0 %copy-start = (bf16[352,4096]{1,0:T(8,128)(2,1)S(1)}, bf16[352,4096]{1,0:T(8,128)(2,1)}, u32[]{:S(2)}) copy-start(bf16[352,4096]{1,0:T(8,128)(2,1)} %param.23) | copy-start | bytes 8650756
  6.5 107.7 %all-gather.3.cloned.1.call-start = ((), (), s32[]{:S(2)}) async-start(), calls=%async_computation.4 | async-start | bytes 8921088 | tf_op jit(solution)/shard_map/all_gather | solution.py:174
  13.4 108.8 %copy-start.3 = (bf16[4096,32]{0,1:T(8,128)(2,1)S(1)}, bf16[4096,32]{0,1:T(8,128)(2,1)}, u32[]{:S(2)}) copy-start(bf16[4096,32]{0,1:T(8,128)(2,1)} %param.18) | copy-start | bytes 786436
  13.4 108.8 %copy-start.4 = (f32[4096]{0:T(1024)S(1)}, f32[4096]{0:T(1024)}, u32[]{:S(2)}) copy-start(f32[4096]{0:T(1024)} %param.15) | copy-start | bytes 49156
  129.6 24.9 %all-to-all-start = ((bf16[32,2,4,1024]{3,2,1,0:T(4,128)(2,1)}), bf16[32,2,4,1024]{3,2,1,0:T(4,128)(2,1)S(1)}, u32[]{:S(2)}, u32[]{:S(2)}) async-start(bf16[32,2,4,1024]{3,2,1,0:T(4,128)(2,1)} %bitcast.7), calls=%async_computation | async-start | bytes 1048576 | tf_op jit(solution)/shard_map/all_to_all | solution.py:196
  160.6 1.9 copy-start.1
  169.4 77.5 %copy-start.2 = (f32[4096]{0:T(1024)S(1)}, f32[4096]{0:T(1024)}, u32[]{:S(2)}) copy-start(f32[4096]{0:T(1024)} %param.20) | copy-start | bytes 49156
  232.6 13.0 %all-to-all-start.1 = ((bf16[4,16,4096]{2,1,0:T(8,128)(2,1)}), bf16[4,16,4096]{2,1,0:T(8,128)(2,1)}, u32[]{:S(2)}, u32[]{:S(2)}) async-start(bf16[4,16,4096]{2,1,0:T(8,128)(2,1)} %bitcast.10), calls=%async_computation.1 | async-start | bytes 1048576 | tf_op jit(solution)/shard_map/all_to_all | solution.py:124
  236.7 77.2 %all-gather.5.cloned.1.call-start = ((), (), s32[]{:S(2)}) async-start(), calls=%async_computation.5 | async-start | bytes 4718592 | tf_op jit(solution)/shard_map/all_gather | solution.py:129
  393.5 12.5 %all-to-all-start.2 = ((bf16[4,16,4096]{2,1,0:T(8,128)(2,1)}), bf16[4,16,4096]{2,1,0:T(8,128)(2,1)}, u32[]{:S(2)}, u32[]{:S(2)}) async-start(bf16[4,16,4096]{2,1,0:T(8,128)(2,1)} %bitcast.30), calls=%async_computation.2 | async-start | bytes 1048576 | tf_op jit(solution)/shard_map/all_to_all | solution.py:124
  408.9 50.3 %all-to-all-start.3 = ((bf16[32,8,4096]{2,1,0:T(8,128)(2,1)}), bf16[32,8,4096]{2,1,0:T(8,128)(2,1)}, u32[]{:S(2)}, u32[]{:S(2)}) async-start(bf16[32,8,4096]{2,1,0:T(8,128)(2,1)} %select_select_fusion), calls=%async_computation.3 | async-start | bytes 4194304 | tf_op jit(solution)/shard_map/all_to_all | solution.py:258
Sparse Core Ops, SparseCore 0:
  13.5 100.7 all-gather.2
  260.6 53.2 all-gather.4

commit v5 on v4

--- a/solution.py
+++ b/solution.py
@@ -43,74 +43,75 @@
 
 
 MESH_ID = pl.DeviceIdType.MESH
-
-
-def _zring_rs_kernel(n, x_ref, out_ref, recv, sendbuf, send_sem, recv_sem, credit):
+SUB_CHUNKS = 2
+
+
+def _zring_rs_kernel(n, x_ref, out_ref, recv, sendbuf, send_sem, recv_sem):
     me = lax.axis_index("cz")
     right = lax.rem(me + 1, n)
     left = lax.rem(me + n - 1, n)
     half = x_ref.shape[2] // 2
+    piece = x_ref.shape[1] // SUB_CHUNKS
     dest = (right, left)
-    sender = (left, right)
 
     barrier = pltpu.get_barrier_semaphore()
     for neighbour in (left, right):
         pl.semaphore_signal(barrier, inc=1, device_id={"cz": neighbour}, device_id_type=MESH_ID)
     pl.semaphore_wait(barrier, 2)
 
+    def link(d, slot, k, src):
+        return pltpu.make_async_remote_copy(
+            src_ref=src,
+            dst_ref=recv.at[d, slot, k],
+            send_sem=send_sem.at[d, slot, k],
+            recv_sem=recv_sem.at[d, slot, k],
+            device_id={"cz": dest[d]},
+            device_id_type=MESH_ID,
+        )
+
+    sends = []
+    for k in range(SUB_CHUNKS):
+        for d in range(2):
+            first = lax.rem(me + n - 1, n) if d == 0 else lax.rem(me + 1, n)
+            copy = link(d, 0, k, x_ref.at[first, pl.ds(k * piece, piece), pl.ds(d * half, half)])
+            copy.start()
+            sends.append(copy)
     for step in range(n - 1):
-        slot = step % 2
-        copies = []
-        for d in range(2):
-            if step == 0:
-                first = lax.rem(me + n - 1, n) if d == 0 else lax.rem(me + 1, n)
-                src = x_ref.at[first, :, pl.ds(d * half, half)]
-            else:
-                pl.semaphore_wait(credit.at[d], 1)
-                src = sendbuf.at[d, (step - 1) % 2]
-            copy = pltpu.make_async_remote_copy(
-                src_ref=src,
-                dst_ref=recv.at[d, slot],
-                send_sem=send_sem.at[d, slot],
-                recv_sem=recv_sem.at[d, slot],
-                device_id={"cz": dest[d]},
-                device_id_type=MESH_ID,
-            )
-            copy.start()
-            copies.append(copy)
-        for d in range(2):
-            copies[d].wait_recv()
-            if d == 0:
-                chunk = lax.rem(me + 2 * n - step - 2, n)
-            else:
-                chunk = lax.rem(me + step + 2, n)
-            total = recv[d, slot].astype(jnp.float32) + x_ref[chunk, :, pl.ds(d * half, half)].astype(
-                jnp.float32
-            )
-            if step == n - 2:
-                out_ref[:, pl.ds(d * half, half)] = total
-            else:
-                sendbuf[d, slot] = total.astype(sendbuf.dtype)
-            if step <= n - 3:
-                pl.semaphore_signal(credit.at[d], inc=1, device_id={"cz": sender[d]}, device_id_type=MESH_ID)
-        for d in range(2):
-            copies[d].wait_send()
+        for k in range(SUB_CHUNKS):
+            for d in range(2):
+                link(d, step, k, sendbuf.at[d, step, k]).wait_recv()
+                if d == 0:
+                    chunk = lax.rem(me + 2 * n - step - 2, n)
+                else:
+                    chunk = lax.rem(me + step + 2, n)
+                total = recv[d, step, k].astype(jnp.float32) + x_ref[
+                    chunk, pl.ds(k * piece, piece), pl.ds(d * half, half)
+                ].astype(jnp.float32)
+                if step == n - 2:
+                    out_ref[pl.ds(k * piece, piece), pl.ds(d * half, half)] = total
+                else:
+                    sendbuf[d, step, k] = total.astype(sendbuf.dtype)
+                    copy = link(d, step + 1, k, sendbuf.at[d, step, k])
+                    copy.start()
+                    sends.append(copy)
+    for copy in sends:
+        copy.wait_send()
 
 
 def zring_reduce_scatter(x, collective_id):
     n, rows, cols = x.shape
     half = cols // 2
+    piece = rows // SUB_CHUNKS
     return pl.pallas_call(
         functools.partial(_zring_rs_kernel, n),
         out_shape=jax.ShapeDtypeStruct((rows, cols), jnp.float32),
         in_specs=[pl.BlockSpec(memory_space=pltpu.VMEM)],
         out_specs=pl.BlockSpec(memory_space=pltpu.VMEM),
         scratch_shapes=[
-            pltpu.VMEM((2, 2, rows, half), x.dtype),
-            pltpu.VMEM((2, 2, rows, half), x.dtype),
-            pltpu.SemaphoreType.DMA((2, 2)),
-            pltpu.SemaphoreType.DMA((2, 2)),
-            pltpu.SemaphoreType.REGULAR((2,)),
+            pltpu.VMEM((2, n - 1, SUB_CHUNKS, piece, half), x.dtype),
+            pltpu.VMEM((2, n - 1, SUB_CHUNKS, piece, half), x.dtype),
+            pltpu.SemaphoreType.DMA((2, n - 1, SUB_CHUNKS)),
+            pltpu.SemaphoreType.DMA((2, n - 1, SUB_CHUNKS)),
         ],
         compiler_params=pltpu.CompilerParams(collective_id=collective_id, has_side_effects=True),
     )(x)

time: 475 us -> 446 us (0.939)
  Pallas kernels: 124 us -> 93.4 us
    pallas_call x2, Pallas kernels: 124 us -> 93.4 us  [zring_reduce_scatter(): pl.pallas_call(functools.partial(_zring_rs_kernel, n), out_shape=jax.Shap...]
    all_to_all x1, waiting for transfers between devices: 40.4 us -> 47 us  [body(): lax.all_to_all(back, GROUP, 0, 0, tiled=True)]
  transfers between devices with their start and end apart: 6 -> 6, of which waited for: 6 -> 6; matrix products, arithmetic and copies ran while one was open for 3% -> 4% of each run, Pallas kernels for 0% -> 0%
where the time goes in v5:
time: 446 us; the launch traced here: 445 us
  waiting for transfers between devices  218 us (49%)
  Pallas kernels  93.4 us (21%)
  matrix products  35.9 us (8%)
  other arithmetic  27 us (6%)
  starting transfers between devices  22.8 us (5%)
  local copies, waits for them, and re-layouts  20.7 us (5%)
  between operations  13.7 us (3%)
  blocking collectives  13.5 us (3%)
    all_gather x1, waiting for transfers between devices, body(): all_packed = lax.all_gather(packed, GROUP, axis=0, tiled=True)  101 us
    pallas_call x2, Pallas kernels, zring_reduce_scatter(): pl.pallas_call(functools.partial(_zring_rs_kernel, n), out_shape=jax.Shap...  93.4 us
    all_gather x1, waiting for transfers between devices, gather_rows(): lax.all_gather(lax.all_gather(x, 'cy', axis=0, tiled=True), 'cz', axis=0,...  50.5 us
    all_to_all x1, waiting for transfers between devices, body(): lax.all_to_all(back, GROUP, 0, 0, tiled=True)  47 us
    all_gather x1, blocking collectives, gather_rows(): lax.all_gather(x, 'cy', axis=0, tiled=True)  13.5 us
    all_to_all x2, waiting for transfers between devices, reduce_scatter_rows(): over_y = lax.all_to_all(part, 'cy', 0, 0, tiled=True)  10.7 us
    dot_general x1, matrix products, body(): jnp.dot(hidden, down_weight, preferred_element_type=jnp.float32)  9.17 us
  transfers between devices with their start and end apart: 6, of which 6 were waited for; matrix products, arithmetic and copies ran while one was open for 4% of the time, Pallas kernels for 0%

profile of v5, /device:TPU:32, one launch (start us, length us, event | category | flops | bytes accessed | tf_op | source)
XLA Modules:
  0.0 444.8 jit_solution(2292433316607565615)
XLA Ops:
  10.1 2.3 gather_fusion
  13.4 100.8 %all-gather.3.cloned.1.call-done = bf16[1024,4224]{1,0:T(8,128)(2,1)} async-done(((bf16[32,4224]{1,0:T(8,128)(2,1)}), bf16[1024,4224]{1,0:T(8,128)(2,1)}) %all-gather.3.cloned.1.call-update) | async-done | bytes 8650768 | tf_op jit(solution)/shard_map/all_gather | solution.py:175
  114.2 5.1 %fusion = f32[1024]{0:T(1024)S(1)} fusion(bf16[1024,4224]{1,0:T(8,128)(2,1)} %all-gather.3.cloned.1.call-done), kind=kLoop, calls=%fused_computation.7 | loop fusion | flops 12581888 | bytes 8392704 | tf_op jit(solution)/shard_map/reduce_sum | solution.py:24
  122.2 6.2 %fusion.13 = bf16[64,1024]{1,0:T(8,128)(2,1)S(1)} fusion(f32[4096]{0:T(1024)S(1)} %copy-done.4, f32[1024]{0:T(1024)S(1)} %add_rsqrt_fusion, bf16[1024,4224]{1,0:T(8,128)(2,1)} %all-gather.3.cloned.1.call-done, bf16[4096,32]{0,1:T(8,128)(2,1)S(1)} %copy-done.3, bf16[4096,32]{0,1:T(8,128)(2,1)} %param.17), kind=kOutput, calls=%fused_computation.26 | convolution fusion | flops 554762240 | bytes 9064448 | tf_op jit(solution)/shard_map/pd,dc->cp/dot_general | solution.py:190
  129.6 7.6 %all-to-all-start = ((bf16[32,2,4,1024]{3,2,1,0:T(4,128)(2,1)}), bf16[32,2,4,1024]{3,2,1,0:T(4,128)(2,1)S(1)}, u32[]{:S(2)}, u32[]{:S(2)}) async-start(bf16[32,2,4,1024]{3,2,1,0:T(4,128)(2,1)} %bitcast.7), calls=%async_computation | async-start | bytes 1048576 | tf_op jit(solution)/shard_map/all_to_all | solution.py:197
  138.4 7.2 %fusion.9 = f32[1024,128]{0,1:T(8,128)} fusion(bf16[4096,128]{1,0:T(8,128)(2,1)} %param.16, f32[4096]{0:T(1024)S(1)} %copy-done.4, f32[1024]{0:T(1024)S(1)} %add_rsqrt_fusion, bf16[1024,4224]{1,0:T(8,128)(2,1)} %all-gather.3.cloned.1.call-done), kind=kOutput, calls=%fused_computation.22 | convolution fusion | flops 1090519040 | bytes 9981952 | tf_op jit(solution)/shard_map/dot_general | solution.py:187
  145.7 8.7 %all-to-all-done = bf16[32,2,4,1024]{3,2,1,0:T(4,128)(2,1)S(1)} async-done(((bf16[32,2,4,1024]{3,2,1,0:T(4,128)(2,1)}), bf16[32,2,4,1024]{3,2,1,0:T(4,128)(2,1)S(1)}, u32[]{:S(2)}, u32[]{:S(2)}) %all-to-all-start) | async-done | bytes 524320 | tf_op jit(solution)/shard_map/all_to_all | solution.py:197
  158.4 2.2 fusion.41
  164.1 5.3 %convolution_convert_fusion = bf16[512,4096]{1,0:T(8,128)(2,1)} fusion(bf16[128,4096]{1,0:T(8,128)(2,1)} %param.19, bf16[1024,128]{1,0:T(8,128)(2,1)S(1)} %fusion.12, s32[512]{0:T(512)S(1)} %eq.110), kind=kOutput, calls=%fused_computation.10 | convolution fusion | flops 673775616 | bytes 5507072 | tf_op jit(solution)/shard_map/dot_general | solution.py:231
  169.4 45.2 %shard_map.118 = f32[64,4096]{1,0:T(8,128)} custom-call(bf16[8,64,4096]{2,1,0:T(8,128)(2,1)} %bitcast.28), custom_call_target="tpu_custom_call" | custom-call | tf_op jit(solution)/shard_map/pallas_call | solution.py:105
  216.6 4.1 all-to-all-start.1
  221.1 5.3 %gather_fusion.2 = bf16[16,4224]{1,0:T(8,128)(2,1)S(1)} fusion(bf16[1024,4224]{1,0:T(8,128)(2,1)} %all-gather.3.cloned.1.call-done, s32[1024]{0:T(1024)S(1)} %pad_clamp_fusion.2), kind=kCustom, calls=%fused_computation.2 | custom fusion | bytes 270400 | tf_op jit(solution)/shard_map/gather | solution.py:227
  226.5 2.6 all-to-all-done.1
  230.4 13.5 %all_gather.10 = bf16[64,4096]{1,0:T(8,128)(2,1)} all-gather(bf16[16,4096]{1,0:T(8,128)(2,1)S(1)} %multiply_convert_fusion), channel_id=1, replica_groups=mesh['dp'=8,'cy'=4,'cz'=8] {'cy'}, dimensions={0}, use_global_device_ids=true | all-gather | bytes 655360 | tf_op jit(solution)/shard_map/all_gather | solution.py:130
  244.3 50.5 %all-gather.5.cloned.1.call-done = bf16[512,4096]{1,0:T(8,128)(2,1)} async-done(((bf16[64,4096]{1,0:T(8,128)(2,1)}), bf16[512,4096]{1,0:T(8,128)(2,1)}) %all-gather.5.cloned.1.call-update) | async-done | bytes 4194320 | tf_op jit(solution)/shard_map/all_gather | solution.py:130
  294.8 5.6 %fusion.104 = f32[512,352]{0,1:T(8,128)} fusion(bf16[512,4096]{1,0:T(8,128)(2,1)} %all-gather.5.cloned.1.call-done, bf16[4096,352]{0,1:T(8,128)(2,1)} %param.21), kind=kOutput, calls=%fused_computation.205 | convolution fusion | flops 1476395008 | bytes 7798784 | tf_op jit(solution)/shard_map/dot_general | solution.py:239
  300.5 9.2 %convolution_convert_fusion.1 = bf16[512,4096]{1,0:T(8,128)(2,1)} fusion(bf16[352,4096]{1,0:T(8,128)(2,1)S(1)} %copy-done, bf16[512,4096]{1,0:T(8,128)(2,1)} %all-gather.5.cloned.1.call-done, bf16[4096,352]{0,1:T(8,128)(2,1)} %param.22, f32[512,352]{0,1:T(8,128)} %fusion.104), kind=kOutput, calls=%fused_computation.11 | convolution fusion | flops 2955968512 | bytes 14876672 | tf_op jit(solution)/shard_map/dot_general | solution.py:243
  309.6 48.2 %shard_map.119 = f32[64,4096]{1,0:T(8,128)} custom-call(bf16[8,64,4096]{2,1,0:T(8,128)(2,1)} %bitcast.29), custom_call_target="tpu_custom_call" | custom-call | tf_op jit(solution)/shard_map/pallas_call | solution.py:105
  359.9 4.3 all-to-all-start.2
  364.3 8.2 %all-to-all-done.2 = bf16[4,16,4096]{2,1,0:T(8,128)(2,1)} async-done(((bf16[4,16,4096]{2,1,0:T(8,128)(2,1)}), bf16[4,16,4096]{2,1,0:T(8,128)(2,1)}, u32[]{:S(2)}, u32[]{:S(2)}) %all-to-all-start.2) | async-done | bytes 524320 | tf_op jit(solution)/shard_map/all_to_all | solution.py:125
  375.3 6.4 %all-to-all-start.3 = ((bf16[32,8,4096]{2,1,0:T(8,128)(2,1)}), bf16[32,8,4096]{2,1,0:T(8,128)(2,1)}, u32[]{:S(2)}, u32[]{:S(2)}) async-start(bf16[32,8,4096]{2,1,0:T(8,128)(2,1)} %select_select_fusion), calls=%async_computation.3 | async-start | bytes 4194304 | tf_op jit(solution)/shard_map/all_to_all | solution.py:259
  383.3 47.0 %all-to-all-done.3 = bf16[32,8,4096]{2,1,0:T(8,128)(2,1)} async-done(((bf16[32,8,4096]{2,1,0:T(8,128)(2,1)}), bf16[32,8,4096]{2,1,0:T(8,128)(2,1)}, u32[]{:S(2)}, u32[]{:S(2)}) %all-to-all-start.3) | async-done | bytes 2097184 | tf_op jit(solution)/shard_map/all_to_all | solution.py:259
  430.3 5.0 %gather_fusion.4 = bf16[128,4096]{1,0:T(8,128)(2,1)} fusion(bf16[256,4096]{1,0:T(8,128)(2,1)} %bitcast.13, s32[1024]{0:T(1024)S(1)} %pad_clamp_fusion), kind=kCustom, calls=%fused_computation.4 | custom fusion | bytes 2097664 | tf_op jit(solution)/shard_map/gather | solution.py:266
  435.3 2.7 broadcast_select_fusion
  (78 shorter events, 27.8 us)
Async XLA Ops:
  6.5 293.9 %copy-start = (bf16[352,4096]{1,0:T(8,128)(2,1)S(1)}, bf16[352,4096]{1,0:T(8,128)(2,1)}, u32[]{:S(2)}) copy-start(bf16[352,4096]{1,0:T(8,128)(2,1)} %param.23) | copy-start | bytes 8650756
  6.5 107.7 %all-gather.3.cloned.1.call-start = ((), (), s32[]{:S(2)}) async-start(), calls=%async_computation.4 | async-start | bytes 8921088 | tf_op jit(solution)/shard_map/all_gather | solution.py:175
  13.4 108.8 %copy-start.3 = (bf16[4096,32]{0,1:T(8,128)(2,1)S(1)}, bf16[4096,32]{0,1:T(8,128)(2,1)}, u32[]{:S(2)}) copy-start(bf16[4096,32]{0,1:T(8,128)(2,1)} %param.18) | copy-start | bytes 786436
  13.4 108.8 %copy-start.4 = (f32[4096]{0:T(1024)S(1)}, f32[4096]{0:T(1024)}, u32[]{:S(2)}) copy-start(f32[4096]{0:T(1024)} %param.15) | copy-start | bytes 49156
  129.6 24.9 %all-to-all-start = ((bf16[32,2,4,1024]{3,2,1,0:T(4,128)(2,1)}), bf16[32,2,4,1024]{3,2,1,0:T(4,128)(2,1)S(1)}, u32[]{:S(2)}, u32[]{:S(2)}) async-start(bf16[32,2,4,1024]{3,2,1,0:T(4,128)(2,1)} %bitcast.7), calls=%async_computation | async-start | bytes 1048576 | tf_op jit(solution)/shard_map/all_to_all | solution.py:197
  160.6 1.9 copy-start.1
  169.4 61.0 %copy-start.2 = (f32[4096]{0:T(1024)S(1)}, f32[4096]{0:T(1024)}, u32[]{:S(2)}) copy-start(f32[4096]{0:T(1024)} %param.20) | copy-start | bytes 49156
  216.6 12.4 %all-to-all-start.1 = ((bf16[4,16,4096]{2,1,0:T(8,128)(2,1)}), bf16[4,16,4096]{2,1,0:T(8,128)(2,1)}, u32[]{:S(2)}, u32[]{:S(2)}) async-start(bf16[4,16,4096]{2,1,0:T(8,128)(2,1)} %bitcast.10), calls=%async_computation.1 | async-start | bytes 1048576 | tf_op jit(solution)/shard_map/all_to_all | solution.py:125
  220.8 74.1 %all-gather.5.cloned.1.call-start = ((), (), s32[]{:S(2)}) async-start(), calls=%async_computation.5 | async-start | bytes 4718592 | tf_op jit(solution)/shard_map/all_gather | solution.py:130
  359.9 12.5 %all-to-all-start.2 = ((bf16[4,16,4096]{2,1,0:T(8,128)(2,1)}), bf16[4,16,4096]{2,1,0:T(8,128)(2,1)}, u32[]{:S(2)}, u32[]{:S(2)}) async-start(bf16[4,16,4096]{2,1,0:T(8,128)(2,1)} %bitcast.30), calls=%async_computation.2 | async-start | bytes 1048576 | tf_op jit(solution)/shard_map/all_to_all | solution.py:125
  375.3 54.9 %all-to-all-start.3 = ((bf16[32,8,4096]{2,1,0:T(8,128)(2,1)}), bf16[32,8,4096]{2,1,0:T(8,128)(2,1)}, u32[]{:S(2)}, u32[]{:S(2)}) async-start(bf16[32,8,4096]{2,1,0:T(8,128)(2,1)} %select_select_fusion), calls=%async_computation.3 | async-start | bytes 4194304 | tf_op jit(solution)/shard_map/all_to_all | solution.py:259
Sparse Core Ops, SparseCore 0:
  13.5 100.7 all-gather.2
  244.1 50.6 all-gather.4

commit v6 on v5

--- a/solution.py
+++ b/solution.py
@@ -46,18 +46,26 @@
 SUB_CHUNKS = 2
 
 
-def _zring_rs_kernel(n, x_ref, out_ref, recv, sendbuf, send_sem, recv_sem):
-    me = lax.axis_index("cz")
+def _enter(nz, ny):
+    me_z = lax.axis_index("cz")
+    me_y = lax.axis_index("cy")
+    barrier = pltpu.get_barrier_semaphore()
+    for neighbour in (lax.rem(me_z + nz - 1, nz), lax.rem(me_z + 1, nz)):
+        pl.semaphore_signal(barrier, inc=1, device_id={"cz": neighbour}, device_id_type=MESH_ID)
+    for shift in range(1, ny):
+        pl.semaphore_signal(barrier, inc=1, device_id={"cy": lax.rem(me_y + shift, ny)}, device_id_type=MESH_ID)
+    pl.semaphore_wait(barrier, 2 + ny - 1)
+    return me_z, me_y
+
+
+def _rs_kernel(n, ny, x_ref, out_ref, recv, sendbuf, send_sem, recv_sem, zsum, ybuf, yrecv, ysend_sem, yrecv_sem):
+    me, me_y = _enter(n, ny)
     right = lax.rem(me + 1, n)
     left = lax.rem(me + n - 1, n)
     half = x_ref.shape[2] // 2
     piece = x_ref.shape[1] // SUB_CHUNKS
+    own = out_ref.shape[0]
     dest = (right, left)
-
-    barrier = pltpu.get_barrier_semaphore()
-    for neighbour in (left, right):
-        pl.semaphore_signal(barrier, inc=1, device_id={"cz": neighbour}, device_id_type=MESH_ID)
-    pl.semaphore_wait(barrier, 2)
 
     def link(d, slot, k, src):
         return pltpu.make_async_remote_copy(
@@ -88,23 +96,43 @@
                     chunk, pl.ds(k * piece, piece), pl.ds(d * half, half)
                 ].astype(jnp.float32)
                 if step == n - 2:
-                    out_ref[pl.ds(k * piece, piece), pl.ds(d * half, half)] = total
+                    zsum[pl.ds(k * piece, piece), pl.ds(d * half, half)] = total
                 else:
                     sendbuf[d, step, k] = total.astype(sendbuf.dtype)
                     copy = link(d, step + 1, k, sendbuf.at[d, step, k])
                     copy.start()
                     sends.append(copy)
-    for copy in sends:
+    ysends = []
+    for shift in range(1, ny):
+        peer = lax.rem(me_y + shift, ny)
+        ybuf[shift - 1] = zsum[pl.ds(pl.multiple_of(peer * own, own), own), :].astype(ybuf.dtype)
+        copy = pltpu.make_async_remote_copy(
+            src_ref=ybuf.at[shift - 1],
+            dst_ref=yrecv.at[shift - 1],
+            send_sem=ysend_sem.at[shift - 1],
+            recv_sem=yrecv_sem.at[shift - 1],
+            device_id={"cy": peer},
+            device_id_type=MESH_ID,
+        )
+        copy.start()
+        ysends.append(copy)
+    total = zsum[pl.ds(pl.multiple_of(me_y * own, own), own), :]
+    for shift in range(1, ny):
+        ysends[shift - 1].wait_recv()
+        total = total + yrecv[shift - 1].astype(jnp.float32)
+    out_ref[...] = total
+    for copy in sends + ysends:
         copy.wait_send()
 
 
-def zring_reduce_scatter(x, collective_id):
+def reduce_scatter_kernel(x, ny, collective_id):
     n, rows, cols = x.shape
     half = cols // 2
     piece = rows // SUB_CHUNKS
+    own = rows // ny
     return pl.pallas_call(
-        functools.partial(_zring_rs_kernel, n),
-        out_shape=jax.ShapeDtypeStruct((rows, cols), jnp.float32),
+        functools.partial(_rs_kernel, n, ny),
+        out_shape=jax.ShapeDtypeStruct((own, cols), jnp.float32),
         in_specs=[pl.BlockSpec(memory_space=pltpu.VMEM)],
         out_specs=pl.BlockSpec(memory_space=pltpu.VMEM),
         scratch_shapes=[
@@ -112,22 +140,95 @@
             pltpu.VMEM((2, n - 1, SUB_CHUNKS, piece, half), x.dtype),
             pltpu.SemaphoreType.DMA((2, n - 1, SUB_CHUNKS)),
             pltpu.SemaphoreType.DMA((2, n - 1, SUB_CHUNKS)),
+            pltpu.VMEM((rows, cols), jnp.float32),
+            pltpu.VMEM((ny - 1, own, cols), x.dtype),
+            pltpu.VMEM((ny - 1, own, cols), x.dtype),
+            pltpu.SemaphoreType.DMA((ny - 1,)),
+            pltpu.SemaphoreType.DMA((ny - 1,)),
         ],
         compiler_params=pltpu.CompilerParams(collective_id=collective_id, has_side_effects=True),
     )(x)
 
 
-def reduce_scatter_rows(partial, y_size, z_size, collective_id):
-    rows, width = partial.shape
-    own = rows // (y_size * z_size)
-    over_z = zring_reduce_scatter(partial.reshape(z_size, y_size * own, width), collective_id)
-    part = over_z.astype(jnp.bfloat16).reshape(y_size, own, width)
-    over_y = lax.all_to_all(part, "cy", 0, 0, tiled=True)
-    return jnp.sum(over_y.astype(jnp.float32), axis=0)
-
-
-def gather_rows(x):
-    return lax.all_gather(lax.all_gather(x, "cy", axis=0, tiled=True), "cz", axis=0, tiled=True)
+def _ag_kernel(n, ny, x_ref, out_ref, own_sem, ysend_sem, yrecv_sem, send_sem, recv_sem):
+    me, me_y = _enter(n, ny)
+    right = lax.rem(me + 1, n)
+    left = lax.rem(me + n - 1, n)
+    rows = x_ref.shape[0]
+    half = rows // 2
+    dest = (right, left)
+    mine = pltpu.make_async_copy(x_ref, out_ref.at[me, me_y], own_sem.at[0])
+    mine.start()
+    ysends = []
+    for shift in range(1, ny):
+        peer = lax.rem(me_y + shift, ny)
+        copy = pltpu.make_async_remote_copy(
+            src_ref=x_ref,
+            dst_ref=out_ref.at[me, me_y],
+            send_sem=ysend_sem.at[shift - 1],
+            recv_sem=yrecv_sem.at[me_y],
+            device_id={"cy": peer},
+            device_id_type=MESH_ID,
+        )
+        copy.start()
+        ysends.append(copy)
+    mine.wait()
+    for shift in range(1, ny):
+        peer = lax.rem(me_y + shift, ny)
+        pltpu.make_async_remote_copy(
+            src_ref=x_ref,
+            dst_ref=out_ref.at[me, peer],
+            send_sem=ysend_sem.at[shift - 1],
+            recv_sem=yrecv_sem.at[peer],
+            device_id={"cy": peer},
+            device_id_type=MESH_ID,
+        ).wait_recv()
+
+    def link(d, step, idx):
+        rows_here = pl.ds(d * half, half)
+        return pltpu.make_async_remote_copy(
+            src_ref=out_ref.at[idx, :, rows_here],
+            dst_ref=out_ref.at[idx, :, rows_here],
+            send_sem=send_sem.at[d, step],
+            recv_sem=recv_sem.at[d, step],
+            device_id={"cz": dest[d]},
+            device_id_type=MESH_ID,
+        )
+
+    sends = []
+    for step in range(n - 1):
+        for d in range(2):
+            if step > 0:
+                got = lax.rem(me + n - step, n) if d == 0 else lax.rem(me + step, n)
+                link(d, step - 1, got).wait_recv()
+            idx = lax.rem(me + n - step, n) if d == 0 else lax.rem(me + step, n)
+            copy = link(d, step, idx)
+            copy.start()
+            sends.append(copy)
+    for d in range(2):
+        got = lax.rem(me + 1, n) if d == 0 else lax.rem(me + n - 1, n)
+        link(d, n - 2, got).wait_recv()
+    for copy in ysends + sends:
+        copy.wait_send()
+
+
+def all_gather_kernel(x, n, ny, collective_id):
+    rows, cols = x.shape
+    out = pl.pallas_call(
+        functools.partial(_ag_kernel, n, ny),
+        out_shape=jax.ShapeDtypeStruct((n, ny, rows, cols), x.dtype),
+        in_specs=[pl.BlockSpec(memory_space=pltpu.VMEM)],
+        out_specs=pl.BlockSpec(memory_space=pltpu.VMEM),
+        scratch_shapes=[
+            pltpu.SemaphoreType.DMA((1,)),
+            pltpu.SemaphoreType.DMA((ny - 1,)),
+            pltpu.SemaphoreType.DMA((ny,)),
+            pltpu.SemaphoreType.DMA((2, n - 1)),
+            pltpu.SemaphoreType.DMA((2, n - 1)),
+        ],
+        compiler_params=pltpu.CompilerParams(collective_id=collective_id, has_side_effects=True),
+    )(x)
+    return out.reshape(n * ny * rows, cols)
 
 
 def body(
@@ -227,24 +328,16 @@
     own_packed = all_packed[own_flat]
     own_rows = own_packed[:, :width].astype(jnp.float32)
     scale_own = own_packed[:, width + 1].astype(jnp.float32)
-    attn_own = reduce_scatter_rows(
-        jnp.dot(head_out, output_weight, preferred_element_type=jnp.float32).astype(jnp.bfloat16),
-        y_size,
-        z_size,
-        0,
-    )
+    attn_partial = jnp.dot(head_out, output_weight, preferred_element_type=jnp.float32).astype(jnp.bfloat16)
+    attn_own = reduce_scatter_kernel(attn_partial.reshape(z_size, y_size * PICK_DEV, width), y_size, 0)
     mixed_own = own_rows + attn_own
     normed_own = rms_scale(mixed_own, ffn_gain).astype(jnp.bfloat16)
-    normed_ffn = gather_rows(normed_own)
+    normed_ffn = all_gather_kernel(normed_own, z_size, y_size, 2)
     gate_proj = jnp.dot(normed_ffn, gate_weight, preferred_element_type=jnp.float32)
     up_proj = jnp.dot(normed_ffn, up_weight, preferred_element_type=jnp.float32)
     hidden = (jax.nn.silu(gate_proj) * up_proj).astype(jnp.bfloat16)
-    ffn_own = reduce_scatter_rows(
-        jnp.dot(hidden, down_weight, preferred_element_type=jnp.float32).astype(jnp.bfloat16),
-        y_size,
-        z_size,
-        1,
-    )
+    ffn_partial = jnp.dot(hidden, down_weight, preferred_element_type=jnp.float32).astype(jnp.bfloat16)
+    ffn_own = reduce_scatter_kernel(ffn_partial.reshape(z_size, y_size * PICK_DEV, width), y_size, 1)
     final_own = (own_rows + scale_own[:, None] * (attn_own + ffn_own)).astype(jnp.bfloat16)
     own_source = lax.dynamic_slice_in_dim(source, own_start, PICK_DEV, 0)
     targets = jnp.arange(ctx_size, dtype=jnp.int32)[:, None]

time: 446 us -> 416 us (0.933)
  waiting for transfers between devices: 218 us -> 138 us
  Pallas kernels: 93.4 us -> 166 us
  blocking collectives: 13.5 us -> 0 us
  starting transfers between devices: 22.8 us -> 14 us
    pallas_call x2 -> x3, Pallas kernels: 93.4 us -> 166 us  [the longest x2 104 us: reduce_scatter_kernel(): pl.pallas_call(functools.partial(_rs_kernel, n, ny), out_shape=jax.ShapeD...]
    all_gather x1 -> x0, waiting for transfers between devices: 50.5 us -> none  [gather_rows(): lax.all_gather(lax.all_gather(x, 'cy', axis=0, tiled=True), 'cz', axis=0,...]
    all_to_all x1, waiting for transfers between devices: 47 us -> 28.5 us  [body(): lax.all_to_all(back, GROUP, 0, 0, tiled=True)]
    all_gather x1 -> x0, blocking collectives: 13.5 us -> none  [gather_rows(): lax.all_gather(x, 'cy', axis=0, tiled=True)]
    all_to_all x2 -> x0, waiting for transfers between devices: 10.7 us -> none  [reduce_scatter_rows(): over_y = lax.all_to_all(part, 'cy', 0, 0, tiled=True)]
    all_to_all x2 -> x0, starting transfers between devices: 8.43 us -> none  [reduce_scatter_rows(): over_y = lax.all_to_all(part, 'cy', 0, 0, tiled=True)]
  transfers between devices with their start and end apart: 6 -> 3, of which waited for: 6 -> 3; matrix products, arithmetic and copies ran while one was open for 4% -> 2% of each run, Pallas kernels for 0% -> 0%
where the time goes in v6:
time: 416 us; the launch traced here: 413 us
  Pallas kernels  166 us (40%)
  waiting for transfers between devices  138 us (33%)
  matrix products  36 us (9%)
  other arithmetic  25.1 us (6%)
  local copies, waits for them, and re-layouts  20.5 us (5%)
  starting transfers between devices  14 us (3%)
  between operations  13.7 us (3%)
    pallas_call x2, Pallas kernels, reduce_scatter_kernel(): pl.pallas_call(functools.partial(_rs_kernel, n, ny), out_shape=jax.ShapeD...  104 us
    all_gather x1, waiting for transfers between devices, body(): all_packed = lax.all_gather(packed, GROUP, axis=0, tiled=True)  101 us
    pallas_call x1, Pallas kernels, all_gather_kernel(): pl.pallas_call(functools.partial(_ag_kernel, n, ny), out_shape=jax.ShapeD...  62.2 us
    all_to_all x1, waiting for transfers between devices, body(): lax.all_to_all(back, GROUP, 0, 0, tiled=True)  28.5 us
    dot_general x1, matrix products, body(): jnp.dot(hidden, down_weight, preferred_element_type=jnp.float32)  9.13 us
    all_to_all x1, waiting for transfers between devices, body(): got = lax.all_to_all(send, GROUP, 0, 0, tiled=True)  8.78 us
  transfers between devices with their start and end apart: 3, of which 3 were waited for; matrix products, arithmetic and copies ran while one was open for 2% of the time, Pallas kernels for 0%

profile of v6, /device:TPU:32, one launch (start us, length us, event | category | flops | bytes accessed | tf_op | source)
XLA Modules:
  0.0 413.3 jit_solution(18084136225425885129)
XLA Ops:
  10.1 2.3 gather_fusion
  13.4 100.8 %all-gather.2.cloned.1.call-done = bf16[1024,4224]{1,0:T(8,128)(2,1)} async-done(((bf16[32,4224]{1,0:T(8,128)(2,1)}), bf16[1024,4224]{1,0:T(8,128)(2,1)}) %all-gather.2.cloned.1.call-update) | async-done | bytes 8650768 | tf_op jit(solution)/shard_map/all_gather | solution.py:276
  114.2 5.1 %fusion = f32[1024]{0:T(1024)S(1)} fusion(bf16[1024,4224]{1,0:T(8,128)(2,1)} %all-gather.2.cloned.1.call-done), kind=kLoop, calls=%fused_computation.7 | loop fusion | flops 12581888 | bytes 8392704 | tf_op jit(solution)/shard_map/reduce_sum | solution.py:24
  122.5 5.3 %gather_fusion.2 = bf16[16,4224]{1,0:T(8,128)(2,1)S(1)} fusion(bf16[1024,4224]{1,0:T(8,128)(2,1)} %all-gather.2.cloned.1.call-done, s32[1024]{0:T(1024)S(1)} %pad_clamp_fusion.2), kind=kCustom, calls=%fused_computation.2 | custom fusion | bytes 270400 | tf_op jit(solution)/shard_map/gather | solution.py:328
  128.0 6.3 %fusion.13 = bf16[64,1024]{1,0:T(8,128)(2,1)S(1)} fusion(f32[4096]{0:T(1024)S(1)} %copy-done.4, f32[1024]{0:T(1024)S(1)} %add_rsqrt_fusion, bf16[1024,4224]{1,0:T(8,128)(2,1)} %all-gather.2.cloned.1.call-done, bf16[4096,32]{0,1:T(8,128)(2,1)} %param.18, bf16[4096,32]{0,1:T(8,128)(2,1)} %param.17), kind=kOutput, calls=%fused_computation.26 | convolution fusion | flops 554762240 | bytes 9064448 | tf_op jit(solution)/shard_map/pd,dc->cp/dot_general | solution.py:291
  135.4 7.7 %all-to-all-start = ((bf16[32,2,4,1024]{3,2,1,0:T(4,128)(2,1)}), bf16[32,2,4,1024]{3,2,1,0:T(4,128)(2,1)}, u32[]{:S(2)}, u32[]{:S(2)}) async-start(bf16[32,2,4,1024]{3,2,1,0:T(4,128)(2,1)} %bitcast.31), calls=%async_computation | async-start | bytes 1048576 | tf_op jit(solution)/shard_map/all_to_all | solution.py:298
  144.4 7.3 %fusion.9 = f32[1024,128]{0,1:T(8,128)} fusion(bf16[4096,128]{1,0:T(8,128)(2,1)} %param.16, f32[4096]{0:T(1024)S(1)} %copy-done.4, f32[1024]{0:T(1024)S(1)} %add_rsqrt_fusion, bf16[1024,4224]{1,0:T(8,128)(2,1)} %all-gather.2.cloned.1.call-done), kind=kOutput, calls=%fused_computation.22 | convolution fusion | flops 1090519040 | bytes 9981952 | tf_op jit(solution)/shard_map/dot_general | solution.py:288
  151.6 8.8 %all-to-all-done = bf16[32,2,4,1024]{3,2,1,0:T(4,128)(2,1)} async-done(((bf16[32,2,4,1024]{3,2,1,0:T(4,128)(2,1)}), bf16[32,2,4,1024]{3,2,1,0:T(4,128)(2,1)}, u32[]{:S(2)}, u32[]{:S(2)}) %all-to-all-start) | async-done | bytes 524320 | tf_op jit(solution)/shard_map/all_to_all | solution.py:298
  160.4 2.0 slice_convert_fusion
  162.4 2.0 reshape.553
  165.1 2.3 fusion.41
  169.4 1.6 fusion.12
  170.9 5.2 %convolution_convert_fusion = bf16[512,4096]{1,0:T(8,128)(2,1)} fusion(bf16[128,4096]{1,0:T(8,128)(2,1)} %param.19, bf16[1024,128]{1,0:T(8,128)(2,1)S(1)} %fusion.12, s32[512]{0:T(512)S(1)} %eq.110), kind=kOutput, calls=%fused_computation.10 | convolution fusion | flops 673775616 | bytes 5507072 | tf_op jit(solution)/shard_map/dot_general | solution.py:331
  176.2 51.4 %shard_map.118 = f32[16,4096]{1,0:T(8,128)} custom-call(bf16[8,64,4096]{2,1,0:T(8,128)(2,1)} %bitcast.27), custom_call_target="tpu_custom_call" | custom-call | tf_op jit(solution)/shard_map/pallas_call | solution.py:133
  228.7 1.7 multiply_convert_fusion.x_ref
  230.4 62.2 %shard_map.119 = bf16[8,4,16,4096]{3,2,1,0:T(8,128)(2,1)} custom-call(bf16[16,4096]{1,0:T(8,128)(2,1)} %multiply_convert_fusion.x_ref), custom_call_target="tpu_custom_call" | custom-call | tf_op jit(solution)/shard_map/pallas_call | solution.py:217
  292.6 5.6 %fusion.104 = f32[512,352]{0,1:T(8,128)} fusion(bf16[512,4096]{1,0:T(8,128)(2,1)} %bitcast.28, bf16[4096,352]{0,1:T(8,128)(2,1)} %param.21), kind=kOutput, calls=%fused_computation.203 | convolution fusion | flops 1476395008 | bytes 7798784 | tf_op jit(solution)/shard_map/dot_general | solution.py:336
  298.3 9.1 %convolution_convert_fusion.1 = bf16[512,4096]{1,0:T(8,128)(2,1)} fusion(bf16[352,4096]{1,0:T(8,128)(2,1)S(1)} %copy-done, bf16[512,4096]{1,0:T(8,128)(2,1)} %bitcast.29, bf16[4096,352]{0,1:T(8,128)(2,1)} %param.22, f32[512,352]{0,1:T(8,128)} %fusion.104), kind=kOutput, calls=%fused_computation.11 | convolution fusion | flops 2955968512 | bytes 14876672 | tf_op jit(solution)/shard_map/dot_general | solution.py:339
  307.4 52.2 %shard_map.120 = f32[16,4096]{1,0:T(8,128)} custom-call(bf16[8,64,4096]{2,1,0:T(8,128)(2,1)} %bitcast.30), custom_call_target="tpu_custom_call" | custom-call | tf_op jit(solution)/shard_map/pallas_call | solution.py:133
  360.7 1.7 select_select_fusion
  362.4 6.3 %all-to-all-start.1 = ((bf16[32,8,4096]{2,1,0:T(8,128)(2,1)}), bf16[32,8,4096]{2,1,0:T(8,128)(2,1)}, u32[]{:S(2)}, u32[]{:S(2)}) async-start(bf16[32,8,4096]{2,1,0:T(8,128)(2,1)} %select_select_fusion), calls=%async_computation.1 | async-start | bytes 4194304 | tf_op jit(solution)/shard_map/all_to_all | solution.py:352
  370.2 28.5 %all-to-all-done.1 = bf16[32,8,4096]{2,1,0:T(8,128)(2,1)} async-done(((bf16[32,8,4096]{2,1,0:T(8,128)(2,1)}), bf16[32,8,4096]{2,1,0:T(8,128)(2,1)}, u32[]{:S(2)}, u32[]{:S(2)}) %all-to-all-start.1) | async-done | bytes 2097184 | tf_op jit(solution)/shard_map/all_to_all | solution.py:352
  398.7 5.0 %gather_fusion.4 = bf16[128,4096]{1,0:T(8,128)(2,1)} fusion(bf16[256,4096]{1,0:T(8,128)(2,1)} %bitcast.12, s32[1024]{0:T(1024)S(1)} %pad_clamp_fusion), kind=kCustom, calls=%fused_computation.4 | custom fusion | bytes 2097664 | tf_op jit(solution)/shard_map/gather | solution.py:359
  403.8 2.7 broadcast_select_fusion
  (67 shorter events, 16.5 us)
Async XLA Ops:
  6.5 291.7 %copy-start = (bf16[352,4096]{1,0:T(8,128)(2,1)S(1)}, bf16[352,4096]{1,0:T(8,128)(2,1)}, u32[]{:S(2)}) copy-start(bf16[352,4096]{1,0:T(8,128)(2,1)} %param.23) | copy-start | bytes 8650756
  6.5 107.7 %all-gather.2.cloned.1.call-start = ((), (), s32[]{:S(2)}) async-start(), calls=%async_computation.2 | async-start | bytes 8921088 | tf_op jit(solution)/shard_map/all_gather | solution.py:276
  13.4 114.6 %copy-start.4 = (f32[4096]{0:T(1024)S(1)}, f32[4096]{0:T(1024)}, u32[]{:S(2)}) copy-start(f32[4096]{0:T(1024)} %param.15) | copy-start | bytes 49156
  135.4 25.0 %all-to-all-start = ((bf16[32,2,4,1024]{3,2,1,0:T(4,128)(2,1)}), bf16[32,2,4,1024]{3,2,1,0:T(4,128)(2,1)}, u32[]{:S(2)}, u32[]{:S(2)}) async-start(bf16[32,2,4,1024]{3,2,1,0:T(4,128)(2,1)} %bitcast.31), calls=%async_computation | async-start | bytes 1048576 | tf_op jit(solution)/shard_map/all_to_all | solution.py:298
  167.5 1.9 copy-start.2
  170.9 57.8 %copy-start.3 = (f32[4096]{0:T(1024)S(1)}, f32[4096]{0:T(1024)}, u32[]{:S(2)}) copy-start(f32[4096]{0:T(1024)} %param.20) | copy-start | bytes 49156
  307.4 52.2 %copy-start.1 = (f32[16,4096]{1,0:T(8,128)S(1)}, f32[16,4096]{1,0:T(8,128)}, u32[]{:S(2)}) copy-start(f32[16,4096]{1,0:T(8,128)} %shard_map.118) | copy-start | bytes 786436
  362.4 36.4 %all-to-all-start.1 = ((bf16[32,8,4096]{2,1,0:T(8,128)(2,1)}), bf16[32,8,4096]{2,1,0:T(8,128)(2,1)}, u32[]{:S(2)}, u32[]{:S(2)}) async-start(bf16[32,8,4096]{2,1,0:T(8,128)(2,1)} %select_select_fusion), calls=%async_computation.1 | async-start | bytes 4194304 | tf_op jit(solution)/shard_map/all_to_all | solution.py:352
Sparse Core Ops, SparseCore 0:
  13.5 100.7 all-gather.1

commit v7 on v6

--- a/solution.py
+++ b/solution.py
@@ -273,14 +273,22 @@
         jnp.where(lane == 1, padded_gate[:, None], jnp.zeros((), jnp.bfloat16)),
     )
     packed = jnp.concatenate((padded_rows, extra), axis=1)
-    all_packed = lax.all_gather(packed, GROUP, axis=0, tiled=True)
+    lead = MOST // 2
+    first_part = lax.all_gather(packed[:lead], GROUP, axis=0, tiled=True)
+    second_part = all_gather_kernel(packed[lead:], z_size, y_size, 3)
+    all_packed = jnp.concatenate((first_part, second_part), axis=0)
+    slot_ids = jnp.arange(slots, dtype=jnp.int32)
+    part_blk = (slot_ids % (slots // 2)) // lead
+    slot_dev = jnp.where(slot_ids < slots // 2, part_blk, block_dev[part_blk])
     all_index = all_packed[:, width].astype(jnp.int32)
     slot_filled = all_index >= 0
-    counts = jnp.sum(slot_filled.reshape(ctx_size, MOST).astype(jnp.int32), axis=1)
+    per_part = jnp.sum(slot_filled.reshape(2, ctx_size, lead).astype(jnp.int32), axis=2)
+    dev_ids = jnp.arange(ctx_size, dtype=jnp.int32)
+    dev_block = (dev_ids % z_size) * y_size + dev_ids // z_size
+    counts = per_part[0] + per_part[1][dev_block]
     run_ends = jnp.cumsum(counts)
     run_starts = run_ends - counts
-    slot_ids = jnp.arange(slots, dtype=jnp.int32)
-    slot_pos = (slot_ids // MOST) * tok_local + all_index
+    slot_pos = slot_dev * tok_local + all_index
     rope_pos = jnp.where(slot_filled, slot_pos, 0)
     never = jnp.int32(1 << 30)
     mask_pos = jnp.where(slot_filled, slot_pos, never)
@@ -319,7 +327,10 @@
     before = (run_ends[None, :] <= rank_ids[:, None]).astype(jnp.int32)
     source = jnp.sum(before, axis=1)
     offset = rank_ids - jnp.sum(before * counts[None, :], axis=1)
-    flat_row = source * MOST + offset
+    source_block = (source % z_size) * y_size + source // z_size
+    flat_row = jnp.where(
+        offset < lead, source * lead + offset, slots // 2 + source_block * lead + offset - lead
+    )
     flat_blocked = flat_row.reshape(ctx_size, PICK_DEV)[block_dev].reshape(picked_count)
     pick_onehot = (flat_blocked[:, None] == slot_ids[None, :]).astype(jnp.bfloat16)
     head_out = jnp.dot(pick_onehot, head_pad, preferred_element_type=jnp.float32).astype(jnp.bfloat16)

time: 416 us -> 423 us (1.017)
  waiting for transfers between devices: 138 us -> 29 us
  Pallas kernels: 166 us -> 253 us
  other arithmetic: 25.1 us -> 56.9 us
    all_gather x1, waiting for transfers between devices: 101 us -> 0.02 us  [body(): first_part = lax.all_gather(packed[:lead], GROUP, axis=0, tiled=True)]
    pallas_call x1 -> x2, Pallas kernels: 62.2 us -> 147 us  [all_gather_kernel(): pl.pallas_call(functools.partial(_ag_kernel, n, ny), out_shape=jax.ShapeD...]
    gather x0 -> x28, other arithmetic: none -> 25.4 us  [the longest x27 25.4 us: body(): slot_dev = jnp.where(slot_ids < slots // 2, part_blk, block_dev[part_blk])]
    all_to_all x1, waiting for transfers between devices: 8.78 us -> 0.01 us  [body(): got = lax.all_to_all(send, GROUP, 0, 0, tiled=True)]
    concatenate x0 -> x1, other arithmetic: none -> 7.42 us  [body(): all_packed = jnp.concatenate((first_part, second_part), axis=0)]
  transfers between devices with their start and end apart: 3 -> 3, of which waited for: 3 -> 1; matrix products, arithmetic and copies ran while one was open for 2% -> 12% of each run, Pallas kernels for 0% -> 20%
where the time goes in v7:
time: 423 us; the launch traced here: 422 us
  Pallas kernels  253 us (60%)
  other arithmetic  56.9 us (13%)
  matrix products  32.4 us (8%)
  waiting for transfers between devices  29 us (7%)
  local copies, waits for them, and re-layouts  23.3 us (6%)
  between operations  13.8 us (3%)
  starting transfers between devices  13.3 us (3%)
    pallas_call x2, Pallas kernels, all_gather_kernel(): pl.pallas_call(functools.partial(_ag_kernel, n, ny), out_shape=jax.ShapeD...  147 us
    pallas_call x2, Pallas kernels, reduce_scatter_kernel(): pl.pallas_call(functools.partial(_rs_kernel, n, ny), out_shape=jax.ShapeD...  106 us
    all_to_all x1, waiting for transfers between devices, body(): lax.all_to_all(back, GROUP, 0, 0, tiled=True)  29 us
    gather x27, other arithmetic, body(): slot_dev = jnp.where(slot_ids < slots // 2, part_blk, block_dev[part_blk])  25.4 us
    dot_general x1, matrix products, body(): jnp.dot(hidden, down_weight, preferred_element_type=jnp.float32)  9.13 us
  transfers between devices with their start and end apart: 3, of which 1 were waited for; matrix products, arithmetic and copies ran while one was open for 12% of the time, Pallas kernels for 20%

profile of v7, /device:TPU:32, one launch (start us, length us, event | category | flops | bytes accessed | tf_op | source)
XLA Modules:
  0.0 422.0 jit_solution(412643957632801899)
XLA Ops:
  10.1 2.3 gather_fusion
  19.9 4.5 %select_reduce_fusion = s32[1024]{0:T(1024)S(1)} fusion(s32[]{:T(128)} %bitcast.36, s32[]{:T(128)} %bitcast.37, s32[]{:T(128)} %bitcast.38, s32[]{:T(128)} %bitcast.39, s32[]{:T(128)} %bitcast.40, s32[]{:T(128)} %bitcast.42, s32[]{:T(128)} %bitcast.41), kind=kLoop, calls=%fused_computation.50 | loop fusion | flops 36864 | bytes 4124 | tf_op jit(solution)/shard_map/gather | solution.py:282
  24.4 15.8 %select_select_fusion.2 = s32[1024]{0:T(1024)S(1)} fusion(pred[1024]{0:T(1024)(128)(4,1)S(1)} %compare_reduce_fusion, pred[1024]{0:T(1024)(128)(4,1)S(1)} %compare_reduce_fusion.1, pred[1024]{0:T(1024)(128)(4,1)S(1)} %compare_reduce_fusion.2, pred[1024]{0:T(1024)(128)(4,1)S(1)} %compare_reduce_fusion.3, pred[1024]{0:T(1024)(128)(4,1)S(1)} %compare_reduce_fusion.4, ...), kind=kLoop, calls=%fused_computation.216 | loop fusion | flops 25600 | bytes 33892 | tf_op jit(solution)/shard_map/gather | solution.py:282
  40.5 85.5 %shard_map.118 = bf16[8,4,16,4224]{3,2,1,0:T(8,128)(2,1)} custom-call(bf16[16,4224]{1,0:T(8,128)(2,1)} %get-tuple-element.21.x_ref), custom_call_target="tpu_custom_call" | custom-call | tf_op jit(solution)/shard_map/pallas_call | solution.py:217
  129.5 4.9 %fusion = (f32[1024]{0:T(1024)S(1)}, bf16[1024,4096]{1,0:T(8,128)(2,1)S(1)}) fusion(bf16[512,4224]{1,0:T(8,128)(2,1)} %bitcast.79, bf16[512,4224]{1,0:T(8,128)(2,1)} %all-gather.2.cloned.1.call-done), kind=kLoop, calls=%fused_computation.8 | loop fusion | flops 29359104 | bytes 17043456 | tf_op jit(solution)/shard_map/reduce_sum | solution.py:24
  134.5 2.8 fusion.15
  138.8 5.7 %all-to-all-start = ((bf16[32,2,4,1024]{3,2,1,0:T(4,128)(2,1)}), bf16[32,2,4,1024]{3,2,1,0:T(4,128)(2,1)}, u32[]{:S(2)}, u32[]{:S(2)}) async-start(bf16[32,2,4,1024]{3,2,1,0:T(4,128)(2,1)} %bitcast.46), calls=%async_computation | async-start | bytes 1048576 | tf_op jit(solution)/shard_map/all_to_all | solution.py:306
  144.6 7.4 %pad_maximum_fusion = bf16[1024,4224]{1,0:T(8,128)(2,1)} fusion(bf16[512,4224]{1,0:T(8,128)(2,1)} %bitcast.80, bf16[512,4224]{1,0:T(8,128)(2,1)} %all-gather.2.cloned.1.call-done), kind=kLoop, calls=%fused_computation.13 | loop fusion | flops 17301504 | bytes 17301504 | tf_op jit(solution)/shard_map/concatenate | solution.py:279
  152.0 5.3 %gather_fusion.3 = bf16[16,4224]{1,0:T(8,128)(2,1)S(1)} fusion(bf16[1024,4224]{1,0:T(8,128)(2,1)} %pad_maximum_fusion, s32[1024]{0:T(1024)S(1)} %pad_clamp_fusion.2), kind=kCustom, calls=%fused_computation.3 | custom fusion | bytes 270400 | tf_op jit(solution)/shard_map/gather | solution.py:339
  158.3 7.2 %fusion.8 = f32[1024,128]{0,1:T(8,128)} fusion(bf16[4096,128]{1,0:T(8,128)(2,1)} %param.16, bf16[1024,4096]{1,0:T(8,128)(2,1)} %copy-done.1, f32[4096]{0:T(1024)S(1)} %copy-done.7, f32[1024]{0:T(1024)S(1)} %add_rsqrt_fusion), kind=kOutput, calls=%fused_computation.25 | convolution fusion | flops 1090519040 | bytes 9981952 | tf_op jit(solution)/shard_map/dot_general | solution.py:296
  165.5 2.0 slice_convert_fusion
  167.4 2.0 reshape.692
  170.2 2.3 fusion.45
  176.1 5.2 %convolution_convert_fusion = bf16[512,4096]{1,0:T(8,128)(2,1)} fusion(bf16[128,4096]{1,0:T(8,128)(2,1)} %param.19, bf16[1024,128]{1,0:T(8,128)(2,1)S(1)} %fusion.13, s32[512]{0:T(512)S(1)} %eq.114), kind=kOutput, calls=%fused_computation.17 | convolution fusion | flops 673775616 | bytes 5507072 | tf_op jit(solution)/shard_map/dot_general | solution.py:342
  181.3 54.3 %shard_map.119 = f32[16,4096]{1,0:T(8,128)} custom-call(bf16[8,64,4096]{2,1,0:T(8,128)(2,1)} %bitcast.81), custom_call_target="tpu_custom_call" | custom-call | tf_op jit(solution)/shard_map/pallas_call | solution.py:133
  236.7 1.7 multiply_convert_fusion.x_ref
  238.4 61.5 %shard_map.120 = bf16[8,4,16,4096]{3,2,1,0:T(8,128)(2,1)} custom-call(bf16[16,4096]{1,0:T(8,128)(2,1)} %multiply_convert_fusion.x_ref), custom_call_target="tpu_custom_call" | custom-call | tf_op jit(solution)/shard_map/pallas_call | solution.py:217
  299.9 5.6 %fusion.143 = f32[512,352]{0,1:T(8,128)} fusion(bf16[512,4096]{1,0:T(8,128)(2,1)} %bitcast.82, bf16[4096,352]{0,1:T(8,128)(2,1)} %param.21), kind=kOutput, calls=%fused_computation.308 | convolution fusion | flops 1476395008 | bytes 7798784 | tf_op jit(solution)/shard_map/dot_general | solution.py:347
  305.6 9.1 %convolution_convert_fusion.1 = bf16[512,4096]{1,0:T(8,128)(2,1)} fusion(bf16[352,4096]{1,0:T(8,128)(2,1)S(1)} %copy-done, bf16[512,4096]{1,0:T(8,128)(2,1)} %bitcast.83, bf16[4096,352]{0,1:T(8,128)(2,1)} %param.22, f32[512,352]{0,1:T(8,128)} %fusion.143), kind=kOutput, calls=%fused_computation.18 | convolution fusion | flops 2955968512 | bytes 14876672 | tf_op jit(solution)/shard_map/dot_general | solution.py:350
  314.7 51.9 %shard_map.121 = f32[16,4096]{1,0:T(8,128)} custom-call(bf16[8,64,4096]{2,1,0:T(8,128)(2,1)} %bitcast.84), custom_call_target="tpu_custom_call" | custom-call | tf_op jit(solution)/shard_map/pallas_call | solution.py:133
  369.3 7.6 %all-to-all-start.1 = ((bf16[32,8,4096]{2,1,0:T(8,128)(2,1)}), bf16[32,8,4096]{2,1,0:T(8,128)(2,1)}, u32[]{:S(2)}, u32[]{:S(2)}) async-start(bf16[32,8,4096]{2,1,0:T(8,128)(2,1)} %select_select_fusion), calls=%async_computation.1 | async-start | bytes 4194304 | tf_op jit(solution)/shard_map/all_to_all | solution.py:363
  378.4 29.0 %all-to-all-done.1 = bf16[32,8,4096]{2,1,0:T(8,128)(2,1)} async-done(((bf16[32,8,4096]{2,1,0:T(8,128)(2,1)}), bf16[32,8,4096]{2,1,0:T(8,128)(2,1)}, u32[]{:S(2)}, u32[]{:S(2)}) %all-to-all-start.1) | async-done | bytes 2097184 | tf_op jit(solution)/shard_map/all_to_all | solution.py:363
  407.4 5.0 %gather_fusion.5 = bf16[128,4096]{1,0:T(8,128)(2,1)} fusion(bf16[256,4096]{1,0:T(8,128)(2,1)} %bitcast.51, s32[1024]{0:T(1024)S(1)} %pad_clamp_fusion), kind=kCustom, calls=%fused_computation.5 | custom fusion | bytes 2097664 | tf_op jit(solution)/shard_map/gather | solution.py:370
  412.5 2.7 broadcast_select_fusion
  (112 shorter events, 26.7 us)
Async XLA Ops:
  6.5 299.0 %copy-start = (bf16[352,4096]{1,0:T(8,128)(2,1)S(1)}, bf16[352,4096]{1,0:T(8,128)(2,1)}, u32[]{:S(2)}) copy-start(bf16[352,4096]{1,0:T(8,128)(2,1)} %param.23) | copy-start | bytes 8650756
  6.5 119.6 %all-gather.2.cloned.1.call-start = ((), (), s32[]{:S(2)}) async-start(), calls=%async_computation.2 | async-start | bytes 4460544 | tf_op jit(solution)/shard_map/all_gather | solution.py:277
  129.5 5.0 %copy-start.5 = (bf16[4096,32]{0,1:T(8,128)(2,1)S(1)}, bf16[4096,32]{0,1:T(8,128)(2,1)}, u32[]{:S(2)}) copy-start(bf16[4096,32]{0,1:T(8,128)(2,1)} %param.18) | copy-start | bytes 786436
  129.5 5.0 %copy-start.6 = (bf16[4096,32]{0,1:T(8,128)(2,1)S(1)}, bf16[4096,32]{0,1:T(8,128)(2,1)}, u32[]{:S(2)}) copy-start(bf16[4096,32]{0,1:T(8,128)(2,1)} %param.17) | copy-start | bytes 786436
  129.5 5.0 %copy-start.7 = (f32[4096]{0:T(1024)S(1)}, f32[4096]{0:T(1024)}, u32[]{:S(2)}) copy-start(f32[4096]{0:T(1024)} %param.15) | copy-start | bytes 49156
  134.4 3.2 copy-start.1
  138.8 26.7 %all-to-all-start = ((bf16[32,2,4,1024]{3,2,1,0:T(4,128)(2,1)}), bf16[32,2,4,1024]{3,2,1,0:T(4,128)(2,1)}, u32[]{:S(2)}, u32[]{:S(2)}) async-start(bf16[32,2,4,1024]{3,2,1,0:T(4,128)(2,1)} %bitcast.46), calls=%async_computation | async-start | bytes 1048576 | tf_op jit(solution)/shard_map/all_to_all | solution.py:306
  172.6 1.9 copy-start.3
  176.0 60.7 %copy-start.4 = (f32[4096]{0:T(1024)S(1)}, f32[4096]{0:T(1024)}, u32[]{:S(2)}) copy-start(f32[4096]{0:T(1024)} %param.20) | copy-start | bytes 49156
  314.7 51.9 %copy-start.2 = (f32[16,4096]{1,0:T(8,128)S(1)}, f32[16,4096]{1,0:T(8,128)}, u32[]{:S(2)}) copy-start(f32[16,4096]{1,0:T(8,128)} %shard_map.119) | copy-start | bytes 786436
  369.3 38.1 %all-to-all-start.1 = ((bf16[32,8,4096]{2,1,0:T(8,128)(2,1)}), bf16[32,8,4096]{2,1,0:T(8,128)(2,1)}, u32[]{:S(2)}, u32[]{:S(2)}) async-start(bf16[32,8,4096]{2,1,0:T(8,128)(2,1)} %select_select_fusion), calls=%async_computation.1 | async-start | bytes 4194304 | tf_op jit(solution)/shard_map/all_to_all | solution.py:363
Sparse Core Ops, SparseCore 0:
  13.5 93.0 all-gather.1
